TPU v7x, 32 devices: a whole 2x2x4 slice. The times are simulated.
32 devices in a mesh: dp: 8 (over z, x), tensor: 4 (over y, core).
Axes of the slice: x: 2, y: 2, z: 4, core: 2. Of those that a mesh axis runs over, the one named last changes fastest.
Arguments:
- layer_in: bfloat16 [1024, 8, 1024], P('tensor', 'dp'), may hold values from -6 to 6
- out_grad: bfloat16 [1024, 8, 1024], P('tensor', 'dp'), may hold values from -6 to 6
- lengths: int32 [8], P('dp'), may hold values from 512 to 1024, as said below
- mamba_x: float32 [1024, 1536], P('dp', 'tensor'), may hold values from -0.1875 to 0.1875
- mamba_z: float32 [1024, 1536], P('dp', 'tensor'), may hold values from -0.1875 to 0.1875
- mamba_step: float32 [1024, 24], P('dp', 'tensor'), may hold values from -0.1875 to 0.1875
- query_proj: float32 [1024, 512], P('dp', 'tensor'), may hold values from -0.25 to 0.25
- key_proj: float32 [1024, 256], P('dp', 'tensor'), may hold values from -0.25 to 0.25
- value_proj: float32 [1024, 256], P('dp', 'tensor'), may hold values from -0.1875 to 0.1875
- mamba_out: float32 [1536, 1024], P('tensor', 'dp'), may hold values from -0.15625 to 0.15625
- attend_out: float32 [512, 1024], P('tensor', 'dp'), may hold values from -3 to 3
- mlp_gate: float32 [1024, 2048], P('dp', 'tensor'), may hold values from -0.1875 to 0.1875
- mlp_up: float32 [1024, 2048], P('dp', 'tensor'), may hold values from -0.1875 to 0.1875
- mlp_down: float32 [2048, 1024], P('tensor', 'dp'), may hold values from -0.125 to 0.125
- state_proj: float32 [1024, 256], P(('dp', 'tensor')), may hold values from -0.1875 to 0.1875
- conv_state: float32 [5, 256], P(None, ('dp', 'tensor')), may hold values from -3 to 3
- norm_gains: float32 [2, 1024], P(None, ('dp', 'tensor')), may hold values from 0.5 to 1.5
- conv_mamba: float32 [5, 1536], P(None, 'tensor'), may hold values from -3 to 3
- step_bias: float32 [24], P('tensor'), may hold values from -3 to -0.5
- decay_log: float32 [24], P('tensor'), may hold values from -4 to 1
- skip_gain: float32 [24], P('tensor'), may hold values from 0.5 to 1.5
Outputs:
- layer_out: bfloat16 [1024, 8, 1024], P('tensor', 'dp')
- in_grad: bfloat16 [1024, 8, 1024], P('tensor', 'dp')
- mamba_x_grad: float32 [1024, 1536], P('dp', 'tensor')
- mamba_z_grad: float32 [1024, 1536], P('dp', 'tensor')
- mamba_step_grad: float32 [1024, 24], P('dp', 'tensor')
- query_proj_grad: float32 [1024, 512], P('dp', 'tensor')
- key_proj_grad: float32 [1024, 256], P('dp', 'tensor')
- value_proj_grad: float32 [1024, 256], P('dp', 'tensor')
- mamba_out_grad: float32 [1536, 1024], P('tensor', 'dp')
- attend_out_grad: float32 [512, 1024], P('tensor', 'dp')
- mlp_gate_grad: float32 [1024, 2048], P('dp', 'tensor')
- mlp_up_grad: float32 [1024, 2048], P('dp', 'tensor')
- mlp_down_grad: float32 [2048, 1024], P('tensor', 'dp')
- state_proj_grad: float32 [1024, 256], P(('dp', 'tensor'))
- conv_state_grad: float32 [5, 256], P(None, ('dp', 'tensor'))
- norm_gains_grad: float32 [2, 1024], P(None, ('dp', 'tensor'))
- conv_mamba_grad: float32 [5, 1536], P(None, 'tensor')
- step_bias_grad: float32 [24], P('tensor')
- decay_log_grad: float32 [24], P('tensor')
- skip_gain_grad: float32 [24], P('tensor')
Inputs may be any that keep to these rules, and one draw needn't show every extreme that they name: `lengths`: the valid tokens of a sequence are its first ones; in every draw one sequence has exactly 1024 and another exactly half of 1024.
All inputs are finite; a program needn't handle non-finite values.
Results may differ from a plain program's by a relative error of at most 0.019.
Values may be sent and summed in bfloat16 or wider, within the bound.
No kernel may reach another device: no remote copies, remote signals or barrier semaphores. Data moves between devices by JAX's collectives and lax.ppermute only.
A program may use at most 128 MiB of HBM per device.

v0:
```python
from functools import reduce

import jax
import jax.numpy as jnp
from jax import lax
from jax.sharding import PartitionSpec as P

HD = 64
ATT_BLOCK = 512
SPAN = 256


epsilon = 1e-05
rotary_base = 100000000000.0
HIGHEST = lax.Precision.HIGHEST


def root_norm(values, gain):
    return values * lax.rsqrt(jnp.mean(values * values, axis=-1, keepdims=True) + epsilon) * gain


def rotary_tables(length, size):
    frequency = rotary_base ** (-2.0 * jnp.arange(size // 2, dtype=jnp.float32) / size)
    angles = jnp.arange(length, dtype=jnp.float32)[:, None] * frequency[None, :]
    return (jnp.cos(angles), jnp.sin(angles))


def rotate_pairs(values, cosine, sine):
    half = values.shape[-1] // 2
    first = values[..., :half]
    second = values[..., half:]
    return jnp.concatenate(
        [first * cosine - second * sine, second * cosine + first * sine], axis=-1
    )


def causal_conv(values, taps):
    width = taps.shape[0] - 1
    length = values.shape[0]
    padded = jnp.pad(values, ((width - 1, 0), (0, 0)))
    total = jnp.broadcast_to(taps[width], values.shape)
    for offset in range(width):
        total = total + padded[offset : offset + length] * taps[offset]
    return total


def scan_block(rate, state, block):
    inputs, steps, entry, readout = block
    size = steps.shape[0]
    logs = jnp.cumsum(steps * rate, axis=0)
    order = jnp.arange(size, dtype=jnp.int32)
    causal = (order[:, None] >= order[None, :])[:, :, None]
    spread = jnp.where(causal, logs[:, None, :] - logs[None, :, :], 0.0)
    decay = jnp.where(causal, jnp.exp(spread), 0.0)
    intersection = jnp.dot(readout, entry.T, precision=HIGHEST)
    mixing = decay * intersection[:, :, None] * steps[None, :, :]
    local = jnp.einsum("tsh,shp->thp", mixing, inputs, precision=HIGHEST)
    carried = (
        jnp.einsum("tn,hpn->thp", readout, state, precision=HIGHEST) * jnp.exp(logs)[:, :, None]
    )
    tail = jnp.exp(logs[-1][None, :] - logs) * steps
    fresh = state * jnp.exp(logs[-1])[:, None, None] + jnp.einsum(
        "sh,shp,sn->hpn", tail, inputs, entry, precision=HIGHEST
    )
    return (fresh, local + carried)


def state_scan(inputs, steps, rate, entry, readout):
    length, heads, size = inputs.shape
    blocks = length // SPAN
    pieces = (
        inputs.reshape(blocks, SPAN, heads, size),
        steps.reshape(blocks, SPAN, heads),
        entry.reshape(blocks, SPAN, entry.shape[1]),
        readout.reshape(blocks, SPAN, readout.shape[1]),
    )
    start = jnp.zeros((heads, size, entry.shape[1]), jnp.float32)
    kept_block = jax.checkpoint(scan_block)

    def stepper(state, block):
        return kept_block(rate, state, block)

    final, outs = lax.scan(stepper, start, pieces)
    return outs.reshape(length, heads, size)


def mamba_core(
    ssm_input,
    ssm_gating,
    ssm_states,
    ssm_steps,
    conv_taps,
    conv_shared,
    step_bias,
    decay_log,
    skip_gain,
):
    length = ssm_input.shape[0]
    heads = step_bias.shape[0]
    inputs = jax.nn.silu(causal_conv(ssm_input, conv_taps)).reshape(length, heads, -1)
    shared = jax.nn.silu(causal_conv(ssm_states, conv_shared))
    states = shared.shape[1] // 2
    steps = jax.nn.softplus(ssm_steps + step_bias)
    rate = -jnp.exp(decay_log)
    result = (
        state_scan(inputs, steps, rate, shared[:, :states], shared[:, states:])
        + skip_gain[None, :, None] * inputs
    )
    return result.reshape(length, -1) * jax.nn.silu(ssm_gating)


def swiglu(gate_part, up_part):
    return jax.nn.silu(gate_part) * up_part


def block_scores(block, keys, start, scale):
    length = keys.shape[0]
    scores = jnp.einsum("qcgd,scd->cgqs", block, keys, preferred_element_type=jnp.float32) * scale
    rows = start + jnp.arange(block.shape[0], dtype=jnp.int32)
    allowed = jnp.arange(length, dtype=jnp.int32)[None, :] <= rows[:, None]
    return jnp.where(allowed, scores, -1e30)


def attend_forward(query, keys, values):
    length, heads, size = query.shape
    kv_heads = keys.shape[1]
    groups = heads // kv_heads
    blocks = length // ATT_BLOCK
    scale = size ** (-0.5)
    grouped = query.reshape(blocks, ATT_BLOCK, kv_heads, groups, size)
    starts = jnp.arange(blocks, dtype=jnp.int32) * ATT_BLOCK

    def one_block(item):
        block, start = item
        scores = block_scores(block, keys, start, scale)
        top = jnp.max(scores, axis=-1, keepdims=True)
        expo = jnp.exp(scores - top)
        total = jnp.sum(expo, axis=-1, keepdims=True)
        chance = (expo / total).astype(jnp.bfloat16)
        result = jnp.einsum("cgqs,scd->qcgd", chance, values, preferred_element_type=jnp.float32)
        return (result, (top + jnp.log(total))[..., 0])

    outs, logsum = lax.map(one_block, (grouped, starts))
    return (outs.reshape(length, heads, size), logsum)


def attend_backward(query, keys, values, logsum, grad_out):
    length, heads, size = query.shape
    kv_heads = keys.shape[1]
    groups = heads // kv_heads
    blocks = length // ATT_BLOCK
    scale = size ** (-0.5)
    grouped = query.reshape(blocks, ATT_BLOCK, kv_heads, groups, size)
    grad_grouped = grad_out.reshape(blocks, ATT_BLOCK, kv_heads, groups, size)
    starts = jnp.arange(blocks, dtype=jnp.int32) * ATT_BLOCK

    def one_block(carry, item):
        key_grad, value_grad = carry
        block, start, block_sum, block_grad = item
        scores = block_scores(block, keys, start, scale)
        chance = jnp.exp(scores - block_sum[..., None])
        grad_chance = jnp.einsum(
            "qcgd,scd->cgqs", block_grad, values, preferred_element_type=jnp.float32
        )
        center = jnp.sum(chance * grad_chance, axis=-1, keepdims=True)
        grad_scores = (chance * (grad_chance - center)).astype(jnp.bfloat16)
        query_grad = (
            jnp.einsum("cgqs,scd->qcgd", grad_scores, keys, preferred_element_type=jnp.float32)
            * scale
        )
        key_grad = (
            key_grad
            + jnp.einsum("cgqs,qcgd->scd", grad_scores, block, preferred_element_type=jnp.float32)
            * scale
        )
        value_grad = value_grad + jnp.einsum(
            "cgqs,qcgd->scd",
            chance.astype(jnp.bfloat16),
            block_grad,
            preferred_element_type=jnp.float32,
        )
        return ((key_grad, value_grad), query_grad)

    zeros = jnp.zeros((length, kv_heads, size), jnp.float32)
    (key_grad, value_grad), query_grad = lax.scan(
        one_block, (zeros, zeros), (grouped, starts, logsum, grad_grouped)
    )
    return (query_grad.reshape(length, heads, size), key_grad, value_grad)


def widen(local, ranks, rank, axis):
    size = local.shape[axis]
    shape = list(local.shape)
    shape[axis] = size * ranks
    return lax.dynamic_update_slice_in_dim(
        jnp.zeros(tuple(shape), jnp.float32), local, rank * size, axis
    )


def body(
    layer_in,
    out_grad,
    lengths,
    mamba_x,
    mamba_z,
    mamba_step,
    query_proj,
    key_proj,
    value_proj,
    mamba_out,
    attend_out,
    mlp_gate,
    mlp_up,
    mlp_down,
    state_proj,
    conv_state,
    norm_gains,
    conv_mamba,
    step_bias,
    decay_log,
    skip_gain,
):
    low_type = jnp.bfloat16
    ranks = lax.axis_size("tensor")
    rank = lax.axis_index("tensor")
    rows_local, seq_count, width = layer_in.shape
    length = rows_local * ranks
    token_rows = length * seq_count
    (
        mamba_input,
        mamba_gating,
        mamba_steps,
        query_weight,
        key_weight,
        value_weight,
        mamba_output,
        attend_weight,
        gate_weight,
        up_weight,
        down_weight,
    ) = (
        lax.all_gather(mamba_x.astype(low_type), "dp", axis=0, tiled=True),
        lax.all_gather(mamba_z.astype(low_type), "dp", axis=0, tiled=True),
        lax.all_gather(mamba_step.astype(low_type), "dp", axis=0, tiled=True),
        lax.all_gather(query_proj.astype(low_type), "dp", axis=0, tiled=True),
        lax.all_gather(key_proj.astype(low_type), "dp", axis=0, tiled=True),
        lax.all_gather(value_proj.astype(low_type), "dp", axis=0, tiled=True),
        lax.all_gather(mamba_out.astype(low_type), "dp", axis=1, tiled=True),
        lax.all_gather(attend_out.astype(low_type), "dp", axis=1, tiled=True),
        lax.all_gather(mlp_gate.astype(low_type), "dp", axis=0, tiled=True),
        lax.all_gather(mlp_up.astype(low_type), "dp", axis=0, tiled=True),
        lax.all_gather(mlp_down.astype(low_type), "dp", axis=1, tiled=True),
    )
    state_master, conv_shared, gain_pair = (
        lax.all_gather(state_proj, ("dp", "tensor"), axis=0, tiled=True),
        lax.all_gather(conv_state, ("dp", "tensor"), axis=1, tiled=True),
        lax.all_gather(norm_gains, ("dp", "tensor"), axis=1, tiled=True),
    )
    state_weight = state_master.astype(low_type)
    local_rows = rank * rows_local + jnp.arange(rows_local, dtype=jnp.int32)
    valid = (local_rows[:, None] < lengths[None, :]).astype(jnp.float32)[:, :, None]
    inputs = layer_in.astype(jnp.float32)
    normed_one, norm_one_back = jax.vjp(root_norm, inputs, gain_pair[0])
    rows_one = lax.all_gather(normed_one.astype(low_type), "tensor", axis=0, tiled=True)
    flat_one = rows_one.reshape(token_rows, width)

    def project(weight):
        return jnp.dot(flat_one, weight, preferred_element_type=jnp.float32).reshape(
            length, seq_count, weight.shape[1]
        )

    core = jax.vmap(mamba_core, in_axes=(1, 1, 1, 1, None, None, None, None, None), out_axes=1)
    ssm_out, core_back = jax.vjp(
        core,
        project(mamba_input),
        project(mamba_gating),
        project(state_weight),
        project(mamba_steps),
        conv_mamba,
        conv_shared,
        step_bias,
        decay_log,
        skip_gain,
    )
    ssm_low = ssm_out.astype(low_type)
    cosine, sine = rotary_tables(length, HD)

    def turn(pre):
        shaped = pre.reshape(length, seq_count, pre.shape[2] // HD, HD)
        return rotate_pairs(shaped, cosine[:, None, None, :], sine[:, None, None, :])

    query_full, query_back = jax.vjp(turn, project(query_weight))
    keys_full, keys_back = jax.vjp(turn, project(key_weight))
    query = query_full.astype(low_type)
    keys = keys_full.astype(low_type)
    values = project(value_weight).reshape(length, seq_count, -1, HD).astype(low_type)
    attend = jax.vmap(attend_forward, in_axes=(1, 1, 1), out_axes=(1, 0))
    att_out, logsum = attend(query, keys, values)
    att_low = att_out.reshape(length, seq_count, -1).astype(low_type)
    mixed = lax.psum_scatter(
        (
            jnp.einsum("lsc,cd->lsd", ssm_low, mamba_output, preferred_element_type=jnp.float32)
            + jnp.einsum("lsc,cd->lsd", att_low, attend_weight, preferred_element_type=jnp.float32)
        ).astype(jnp.bfloat16),
        "tensor",
        scatter_dimension=0,
        tiled=True,
    ).astype(jnp.float32)
    middle = inputs + mixed
    normed_two, norm_two_back = jax.vjp(root_norm, middle, gain_pair[1])
    rows_two = lax.all_gather(normed_two.astype(low_type), "tensor", axis=0, tiled=True)
    flat_two = rows_two.reshape(token_rows, width)
    gate = jnp.dot(flat_two, gate_weight, preferred_element_type=jnp.float32)
    upward = jnp.dot(flat_two, up_weight, preferred_element_type=jnp.float32)
    hidden_full, glu_back = jax.vjp(swiglu, gate, upward)
    hidden_low = hidden_full.astype(low_type)
    hidden_rows = hidden_low.reshape(length, seq_count, -1)
    ffn = lax.psum_scatter(
        jnp.einsum(
            "lsc,cd->lsd", hidden_rows, down_weight, preferred_element_type=jnp.float32
        ).astype(jnp.bfloat16),
        "tensor",
        scatter_dimension=0,
        tiled=True,
    ).astype(jnp.float32)
    layer_out = (valid * (middle + ffn)).astype(low_type)
    grad_res = valid * out_grad.astype(jnp.float32)
    grad_rows = lax.all_gather(grad_res.astype(low_type), "tensor", axis=0, tiled=True)
    flat_grad = grad_rows.reshape(token_rows, width)
    grad_hidden = jnp.einsum(
        "rd,cd->rc", flat_grad, down_weight, preferred_element_type=jnp.float32
    )
    down_grad = jnp.einsum("rc,rd->cd", hidden_low, flat_grad, preferred_element_type=jnp.float32)
    gate_grad, up_grad = glu_back(grad_hidden)
    gate_low = gate_grad.astype(low_type)
    up_low = up_grad.astype(low_type)
    gate_w_grad = jnp.einsum("rd,rc->dc", flat_two, gate_low, preferred_element_type=jnp.float32)
    up_w_grad = jnp.einsum("rd,rc->dc", flat_two, up_low, preferred_element_type=jnp.float32)
    gate_rows = gate_low.reshape(length, seq_count, -1)
    up_rows = up_low.reshape(length, seq_count, -1)
    grad_two = lax.psum_scatter(
        (
            jnp.einsum("lsc,dc->lsd", gate_rows, gate_weight, preferred_element_type=jnp.float32)
            + jnp.einsum("lsc,dc->lsd", up_rows, up_weight, preferred_element_type=jnp.float32)
        ).astype(jnp.bfloat16),
        "tensor",
        scatter_dimension=0,
        tiled=True,
    ).astype(jnp.float32)
    grad_mid_norm, gain_two_grad = norm_two_back(grad_two)
    grad_mid = grad_res + grad_mid_norm
    mid_rows = lax.all_gather(grad_mid.astype(low_type), "tensor", axis=0, tiled=True)
    flat_mid = mid_rows.reshape(token_rows, width)
    grad_ssm = jnp.einsum(
        "rd,cd->rc", flat_mid, mamba_output, preferred_element_type=jnp.float32
    ).reshape(length, seq_count, -1)
    grad_att = jnp.einsum("rd,cd->rc", flat_mid, attend_weight, preferred_element_type=jnp.float32)
    grad_att = grad_att.astype(low_type).reshape(length, seq_count, -1, HD)
    mix_out_grad = jnp.einsum(
        "rc,rd->cd", ssm_low.reshape(token_rows, -1), flat_mid, preferred_element_type=jnp.float32
    )
    att_out_grad = jnp.einsum(
        "rc,rd->cd", att_low.reshape(token_rows, -1), flat_mid, preferred_element_type=jnp.float32
    )
    (
        input_grad,
        gating_grad,
        states_grad,
        steps_grad,
        conv_taps_grad,
        conv_shared_grad,
        bias_grad,
        decay_grad,
        skip_grad,
    ) = core_back(grad_ssm)
    attend_back = jax.vmap(attend_backward, in_axes=(1, 1, 1, 0, 1), out_axes=1)
    query_grad, keys_grad, values_grad = attend_back(query, keys, values, logsum, grad_att)
    (query_pre_grad,) = query_back(query_grad)
    (keys_pre_grad,) = keys_back(keys_grad)
    values_pre_grad = values_grad.reshape(length, seq_count, -1)
    low_grads = (
        input_grad.astype(low_type),
        gating_grad.astype(low_type),
        steps_grad.astype(low_type),
        query_pre_grad.astype(low_type),
        keys_pre_grad.astype(low_type),
        values_pre_grad.astype(low_type),
        states_grad.astype(low_type),
    )
    weights_in = (
        mamba_input,
        mamba_gating,
        mamba_steps,
        query_weight,
        key_weight,
        value_weight,
        state_weight,
    )

    def norm_one_term():
        terms = [
            jnp.einsum("lsc,dc->lsd", grad_part, weight, preferred_element_type=jnp.float32)
            for grad_part, weight in zip(low_grads, weights_in)
        ]
        return reduce(jnp.add, terms)

    grad_one = lax.psum_scatter(
        norm_one_term().astype(jnp.bfloat16), "tensor", scatter_dimension=0, tiled=True
    ).astype(jnp.float32)

    def weight_grad(grad_part):
        return jnp.einsum(
            "rd,rc->dc",
            flat_one,
            grad_part.reshape(token_rows, -1),
            preferred_element_type=jnp.float32,
        )

    (
        input_w_grad,
        gating_w_grad,
        steps_w_grad,
        query_w_grad,
        key_w_grad,
        value_w_grad,
        state_w_grad,
    ) = [weight_grad(grad_part) for grad_part in low_grads]
    grad_in, gain_one_grad = norm_one_back(grad_one)
    in_grad = (grad_in + grad_mid).astype(low_type)
    gain_grads = jnp.stack([gain_one_grad, gain_two_grad])
    state_sum, conv_state_sum, gain_sum, conv_taps_sum, bias_sum, decay_sum, skip_sum = lax.psum(
        (
            state_w_grad,
            conv_shared_grad,
            gain_grads,
            widen(conv_taps_grad, ranks, rank, 1),
            widen(bias_grad, ranks, rank, 0),
            widen(decay_grad, ranks, rank, 0),
            widen(skip_grad, ranks, rank, 0),
        ),
        ("dp", "tensor"),
    )
    member = lax.axis_index(("dp", "tensor"))
    members = lax.axis_size(("dp", "tensor"))
    state_rows = width // members
    state_proj_grad = lax.dynamic_slice_in_dim(state_sum, member * state_rows, state_rows, 0)
    conv_cols = conv_state_sum.shape[1] // members
    conv_state_grad = lax.dynamic_slice_in_dim(conv_state_sum, member * conv_cols, conv_cols, 1)
    norm_gains_grad = lax.dynamic_slice_in_dim(gain_sum, member * state_rows, state_rows, 1)
    chans = conv_mamba.shape[1]
    heads_local = step_bias.shape[0]
    conv_mamba_grad = lax.dynamic_slice_in_dim(conv_taps_sum, rank * chans, chans, 1)
    step_bias_grad = lax.dynamic_slice_in_dim(bias_sum, rank * heads_local, heads_local, 0)
    decay_log_grad = lax.dynamic_slice_in_dim(decay_sum, rank * heads_local, heads_local, 0)
    skip_gain_grad = lax.dynamic_slice_in_dim(skip_sum, rank * heads_local, heads_local, 0)
    weight_sums = (
        lax.psum_scatter(input_w_grad, "dp", scatter_dimension=0, tiled=True),
        lax.psum_scatter(gating_w_grad, "dp", scatter_dimension=0, tiled=True),
        lax.psum_scatter(steps_w_grad, "dp", scatter_dimension=0, tiled=True),
        lax.psum_scatter(query_w_grad, "dp", scatter_dimension=0, tiled=True),
        lax.psum_scatter(key_w_grad, "dp", scatter_dimension=0, tiled=True),
        lax.psum_scatter(value_w_grad, "dp", scatter_dimension=0, tiled=True),
        lax.psum_scatter(mix_out_grad, "dp", scatter_dimension=1, tiled=True),
        lax.psum_scatter(att_out_grad, "dp", scatter_dimension=1, tiled=True),
        lax.psum_scatter(gate_w_grad, "dp", scatter_dimension=0, tiled=True),
        lax.psum_scatter(up_w_grad, "dp", scatter_dimension=0, tiled=True),
        lax.psum_scatter(down_grad, "dp", scatter_dimension=1, tiled=True),
    )
    (
        mamba_x_grad,
        mamba_z_grad,
        mamba_step_grad,
        query_proj_grad,
        key_proj_grad,
        value_proj_grad,
        mamba_out_grad,
        attend_out_grad,
        mlp_gate_grad,
        mlp_up_grad,
        mlp_down_grad,
    ) = weight_sums
    return (
        layer_out,
        in_grad,
        mamba_x_grad,
        mamba_z_grad,
        mamba_step_grad,
        query_proj_grad,
        key_proj_grad,
        value_proj_grad,
        mamba_out_grad,
        attend_out_grad,
        mlp_gate_grad,
        mlp_up_grad,
        mlp_down_grad,
        state_proj_grad,
        conv_state_grad,
        norm_gains_grad,
        conv_mamba_grad,
        step_bias_grad,
        decay_log_grad,
        skip_gain_grad,
    )


def solution(mesh):
    in_specs = (
        P("tensor", "dp", None),
        P("tensor", "dp", None),
        P("dp"),
        P("dp", "tensor"),
        P("dp", "tensor"),
        P("dp", "tensor"),
        P("dp", "tensor"),
        P("dp", "tensor"),
        P("dp", "tensor"),
        P("tensor", "dp"),
        P("tensor", "dp"),
        P("dp", "tensor"),
        P("dp", "tensor"),
        P("tensor", "dp"),
        P(("dp", "tensor"), None),
        P(None, ("dp", "tensor")),
        P(None, ("dp", "tensor")),
        P(None, "tensor"),
        P("tensor"),
        P("tensor"),
        P("tensor"),
    )
    out_specs = (
        P("tensor", "dp", None),
        P("tensor", "dp", None),
        P("dp", "tensor"),
        P("dp", "tensor"),
        P("dp", "tensor"),
        P("dp", "tensor"),
        P("dp", "tensor"),
        P("dp", "tensor"),
        P("tensor", "dp"),
        P("tensor", "dp"),
        P("dp", "tensor"),
        P("dp", "tensor"),
        P("tensor", "dp"),
        P(("dp", "tensor"), None),
        P(None, ("dp", "tensor")),
        P(None, ("dp", "tensor")),
        P(None, "tensor"),
        P("tensor"),
        P("tensor"),
        P("tensor"),
    )
    return jax.shard_map(body, mesh=mesh, in_specs=in_specs, out_specs=out_specs, check_vma=False)
```

profile of v0, /device:TPU:0, one launch (start us, length us, event | category | flops | bytes accessed | tf_op | source)
XLA Modules:
  0.0 2006.0 jit_solution(9237883846804717250)
XLA Ops:
  9.6 43.6 %all-gather = f32[32,32,2]{1,2,0:T(2,128)S(1)} all-gather(f32[1,32,2]{1,2,0:T(2,128)} %bitcast.1026), channel_id=1, replica_groups=mesh['dp'=8,'tensor'=4] {'dp','tensor'}, dimensions={0}, use_global_device_ids=true | all-gather | bytes 8448 | tf_op jit(solution)/shard_map/all_gather | solution.py:257
  56.0 30.7 %all_gather.62 = bf16[1024,128]{1,0:T(8,128)(2,1)S(1)} all-gather(bf16[128,128]{1,0:T(8,128)(2,1)S(1)} %convert_element_type.226), channel_id=1, replica_groups=mesh['dp'=8,'tensor'=4] {'dp'}, dimensions={0}, use_global_device_ids=true | all-gather | bytes 294912 | tf_op jit(solution)/shard_map/all_gather | solution.py:245
  87.6 36.7 %all_gather.58 = f32[5,256]{0,1:T(8,128)S(1)} all-gather(f32[5,8]{0,1:T(8,128)S(1)} %copy.259), channel_id=1, replica_groups=mesh['dp'=8,'tensor'=4] {'dp','tensor'}, dimensions={1}, use_global_device_ids=true | all-gather | bytes 5280 | tf_op jit(solution)/shard_map/all_gather | solution.py:256
  124.2 26.1 %all_gather.56 = bf16[1024,6]{0,1:T(8,128)(2,1)S(1)} all-gather(bf16[128,6]{0,1:T(8,128)(2,1)S(1)} %convert_element_type.220), channel_id=1, replica_groups=mesh['dp'=8,'tensor'=4] {'dp'}, dimensions={0}, use_global_device_ids=true | all-gather | bytes 13824 | tf_op jit(solution)/shard_map/all_gather | solution.py:244
  150.4 26.3 %all_gather.64 = bf16[1024,64]{0,1:T(8,128)(2,1)S(1)} all-gather(bf16[128,64]{0,1:T(8,128)(2,1)S(1)} %convert_element_type.228), channel_id=1, replica_groups=mesh['dp'=8,'tensor'=4] {'dp'}, dimensions={0}, use_global_device_ids=true | all-gather | bytes 147456 | tf_op jit(solution)/shard_map/all_gather | solution.py:247
  176.6 26.3 %all_gather.63 = bf16[1024,64]{0,1:T(8,128)(2,1)S(1)} all-gather(bf16[128,64]{0,1:T(8,128)(2,1)S(1)} %convert_element_type.227), channel_id=1, replica_groups=mesh['dp'=8,'tensor'=4] {'dp'}, dimensions={0}, use_global_device_ids=true | all-gather | bytes 147456 | tf_op jit(solution)/shard_map/all_gather | solution.py:246
  204.2 26.4 %all_gather.65 = bf16[128,1024]{1,0:T(8,128)(2,1)S(1)} all-gather(bf16[128,128]{1,0:T(8,128)(2,1)S(1)} %convert_element_type.232), channel_id=1, replica_groups=mesh['dp'=8,'tensor'=4] {'dp'}, dimensions={1}, use_global_device_ids=true | all-gather | bytes 294912 | tf_op jit(solution)/shard_map/all_gather | solution.py:249
  232.2 42.4 %all_gather.59 = bf16[1024,256]{1,0:T(8,128)(2,1)} all-gather(bf16[32,256]{1,0:T(8,128)(2,1)S(1)} %convert.69), channel_id=1, replica_groups=mesh['dp'=8,'tensor'=4] {'dp','tensor'}, dimensions={0}, use_global_device_ids=true | all-gather | bytes 540672 | tf_op jit(solution)/shard_map/all_gather | solution.py:255
  274.6 30.0 %all_gather.61 = bf16[384,1024]{1,0:T(8,128)(2,1)} all-gather(bf16[384,128]{1,0:T(8,128)(2,1)S(1)} %convert_element_type.225), channel_id=1, replica_groups=mesh['dp'=8,'tensor'=4] {'dp'}, dimensions={1}, use_global_device_ids=true | all-gather | bytes 884736 | tf_op jit(solution)/shard_map/all_gather | solution.py:248
  304.6 34.6 %all_gather.60 = bf16[1024,384]{1,0:T(8,128)(2,1)} all-gather(bf16[128,384]{1,0:T(8,128)(2,1)S(1)} %convert_element_type.223), channel_id=1, replica_groups=mesh['dp'=8,'tensor'=4] {'dp'}, dimensions={0}, use_global_device_ids=true | all-gather | bytes 884736 | tf_op jit(solution)/shard_map/all_gather | solution.py:243
  339.1 34.2 %all_gather.57 = bf16[1024,384]{1,0:T(8,128)(2,1)} all-gather(bf16[128,384]{1,0:T(8,128)(2,1)S(1)} %convert_element_type.221), channel_id=1, replica_groups=mesh['dp'=8,'tensor'=4] {'dp'}, dimensions={0}, use_global_device_ids=true | all-gather | bytes 884736 | tf_op jit(solution)/shard_map/all_gather | solution.py:242
  378.4 12.0 while.70
  412.4 88.4 %while.73 = (s32[]{:T(128)}, f32[1,6,64,128]{3,2,1,0:T(8,128)S(1)}, f32[4,1,256,6,64]{2,0,4,3,1:T(4,128)}, f32[4,1,6,64,128]{4,3,2,1,0:T(8,128)}, f32[4,1,256,6]...) while((s32[]{:T(128)}, f32[1,6,64,128]{3,2,1,0:T(8,128)S(1)}, ...), condition=%wide.region_4.5_spmd.clone.clone, body=%wide.region_1.4_spmd.clone.clone.sunk | while | flops 707351040 | bytes 5811584 | solution.py:83
  425.3 9.5 dynamic_update_slice.113
  447.3 9.5 dynamic_update_slice.113
  469.2 9.5 dynamic_update_slice.113
  491.2 9.5 dynamic_update_slice.113
  517.1 26.0 %reduce-scatter.16.cloned.1.call-done = bf16[256,1,1024]{2,0,1:T(8,128)(2,1)} async-done(((bf16[1024,1,1024]{2,0,1:T(8,128)(2,1)}), bf16[256,1,1024]{2,0,1:T(8,128)(2,1)}) %reduce-scatter.16.cloned.1.call-update) | async-done | bytes 524304 | tf_op jit(solution)/shard_map/reduce_scatter | solution.py:300
  555.2 23.2 %all-gather.11.cloned.1.call-done = bf16[1024,1,1024]{2,0,1:T(8,128)(2,1)} async-done(((bf16[256,1,1024]{2,0,1:T(8,128)(2,1)}), bf16[1024,1,1024]{2,0,1:T(8,128)(2,1)}) %all-gather.11.cloned.1.call-update) | async-done | bytes 2097168 | tf_op jit(solution)/shard_map/all_gather | solution.py:311
  582.8 38.4 %all-gather.13.cloned.1.call-done = bf16[1024,512]{1,0:T(8,128)(2,1)} async-done(((bf16[128,512]{1,0:T(8,128)(2,1)}), bf16[1024,512]{1,0:T(8,128)(2,1)}) %all-gather.13.cloned.1.call-update) | async-done | bytes 1048592 | tf_op jit(solution)/shard_map/all_gather | solution.py:250
  625.7 36.2 %all-gather.17.cloned.1.call-done = bf16[512,1024]{1,0:T(8,128)(2,1)} async-done(((bf16[512,128]{1,0:T(8,128)(2,1)}), bf16[512,1024]{1,0:T(8,128)(2,1)}) %all-gather.17.cloned.1.call-update) | async-done | bytes 1048592 | tf_op jit(solution)/shard_map/all_gather | solution.py:252
  661.9 23.8 %all-gather.19.cloned.1.call-done = bf16[1024,1,1024]{2,0,1:T(8,128)(2,1)} async-done(((bf16[256,1,1024]{2,0,1:T(8,128)(2,1)}), bf16[1024,1,1024]{2,0,1:T(8,128)(2,1)}) %all-gather.19.cloned.1.call-update) | async-done | bytes 2097168 | tf_op jit(solution)/shard_map/all_gather | solution.py:328
  696.6 31.3 %reduce-scatter.20.cloned.1.call-done = bf16[256,1,1024]{2,0,1:T(8,128)(2,1)} async-done(((bf16[1024,1,1024]{2,0,1:T(8,128)(2,1)}), bf16[256,1,1024]{2,0,1:T(8,128)(2,1)}) %reduce-scatter.20.cloned.1.call-update) | async-done | bytes 524304 | tf_op jit(solution)/shard_map/reduce_scatter | solution.py:341
  732.8 22.4 %all-gather.21.cloned.1.call-done = bf16[1024,1,1024]{2,0,1:T(8,128)(2,1)} async-done(((bf16[256,1,1024]{2,0,1:T(8,128)(2,1)}), bf16[1024,1,1024]{2,0,1:T(8,128)(2,1)}) %all-gather.21.cloned.1.call-update) | async-done | bytes 2097168 | tf_op jit(solution)/shard_map/all_gather | solution.py:352
  759.9 30.3 %while.72 = (s32[]{:T(128)}, f32[1,1024,1,64]{1,3,2,0:T(8,128)S(1)}, f32[1,1024,1,64]{1,3,2,0:T(8,128)}, f32[2,1,512,1,2,64]{2,0,5,4,3,1:T(2,128)}, bf16[2,1,512...) while((s32[]{:T(128)}, ...), condition=%wide.region_30.31_spmd.clone, body=%wide.region_28.30_spmd.clone.sunk | while | flops 687734272 | bytes 36864172 | solution.py:185
  812.7 219.2 %while.71 = (s32[]{:T(128)}, f32[6]{0:T(128)}, f32[1,6,64,128]{3,2,1,0:T(8,128)}, f32[4,1,256,6,64]{2,0,4,3,1:T(4,128)}, f32[4,1,256,6]{2,3,1,0:T(8,128)}, /*ind...) while((s32[]{:T(128)}, f32[6]{0:T(128)}, ...), condition=%wide.region_27.28_spmd.clone, body=%wide.region_14.27_spmd.clone.sunk | while | flops 1670430208 | bytes 15811172 | solution.py:83
  848.1 7.6 reduce-window.74
  857.5 9.5 dynamic_update_slice.110
  903.0 7.6 reduce-window.74
  912.4 9.5 dynamic_update_slice.110
  958.0 7.6 reduce-window.74
  967.4 9.5 dynamic_update_slice.110
  1013.0 7.6 reduce-window.74
  1022.4 9.5 dynamic_update_slice.110
  1114.9 75.7 %all-reduce.31.cloned.1.call-done = f32[1024,256]{1,0:T(8,128)} async-done(((f32[1024,256]{1,0:T(8,128)}), f32[1024,256]{1,0:T(8,128)}) %all-reduce.31.cloned.1.call-update) | async-done | bytes 1048592 | tf_op jit(solution)/shard_map/psum | solution.py:431
  1192.0 31.2 %reduce-scatter.22.cloned.1.call-done = bf16[256,1,1024]{2,0,1:T(8,128)(2,1)} async-done(((bf16[1024,1,1024]{2,0,1:T(8,128)(2,1)}), bf16[256,1,1024]{2,0,1:T(8,128)(2,1)}) %reduce-scatter.22.cloned.1.call-update) | async-done | bytes 524304 | tf_op jit(solution)/shard_map/reduce_scatter | solution.py:407
  1224.7 40.4 %all-reduce.28 = (f32[5,256]{1,0:T(8,128)S(1)}, f32[2,1024]{1,0:T(2,128)S(1)}, f32[5,1536]{1,0:T(8,128)S(1)}, f32[24]{0:T(128)S(1)}, f32[24]{0:T(128)S(1)}, /*index=5*/f32[24]{0:T(128)S(1)}) all-reduce(f32[5,256]{1,0:T(8,128)S(1)} %pad_add_fusion.6, ...), channel_id=1, replica_groups=mesh['dp'=8,'tensor'=4] {'dp','tensor'}, use_global_device_ids=true, to_apply=%region_50.51 | all-reduce | flops 11080 | bytes 88640 | tf_op jit(solution)/shard_map/psum | solution.py:431
  1271.9 57.7 %reduce-scatter.44.cloned.1.call-done = f32[512,128]{1,0:T(8,128)} async-done(((f32[512,1024]{1,0:T(8,128)}), f32[512,128]{1,0:T(8,128)}) %reduce-scatter.44.cloned.1.call-update) | async-done | bytes 262160 | tf_op jit(solution)/shard_map/reduce_scatter | solution.py:467
  1329.7 71.2 %reduce-scatter.40.cloned.1.call-done = f32[128,512]{1,0:T(8,128)} async-done(((f32[1024,512]{1,0:T(8,128)}), f32[128,512]{1,0:T(8,128)}) %reduce-scatter.40.cloned.1.call-update) | async-done | bytes 262160 | tf_op jit(solution)/shard_map/reduce_scatter | solution.py:465
  1400.9 71.5 %reduce-scatter.42.cloned.1.call-done = f32[128,512]{1,0:T(8,128)} async-done(((f32[1024,512]{1,0:T(8,128)}), f32[128,512]{1,0:T(8,128)}) %reduce-scatter.42.cloned.1.call-update) | async-done | bytes 262160 | tf_op jit(solution)/shard_map/reduce_scatter | solution.py:466
  1472.4 57.3 %reduce-scatter.28.cloned.1.call-done = f32[128,6]{0,1:T(8,128)} async-done(((f32[1024,6]{0,1:T(8,128)}), f32[128,6]{0,1:T(8,128)}) %reduce-scatter.28.cloned.1.call-update) | async-done | bytes 3088 | tf_op jit(solution)/shard_map/reduce_scatter | solution.py:459
  1529.7 65.3 %reduce-scatter.32.cloned.1.call-done = f32[128,64]{0,1:T(8,128)} async-done(((f32[1024,64]{0,1:T(8,128)}), f32[128,64]{0,1:T(8,128)}) %reduce-scatter.32.cloned.1.call-update) | async-done | bytes 32784 | tf_op jit(solution)/shard_map/reduce_scatter | solution.py:461
  1594.9 65.4 %reduce-scatter.34.cloned.1.call-done = f32[128,64]{0,1:T(8,128)} async-done(((f32[1024,64]{0,1:T(8,128)}), f32[128,64]{0,1:T(8,128)}) %reduce-scatter.34.cloned.1.call-update) | async-done | bytes 32784 | tf_op jit(solution)/shard_map/reduce_scatter | solution.py:462
  1660.4 66.2 %reduce-scatter.38.cloned.1.call-done = f32[128,128]{1,0:T(8,128)} async-done(((f32[128,1024]{1,0:T(8,128)}), f32[128,128]{1,0:T(8,128)}) %reduce-scatter.38.cloned.1.call-update) | async-done | bytes 65552 | tf_op jit(solution)/shard_map/reduce_scatter | solution.py:464
  1726.6 65.6 %reduce-scatter.30.cloned.1.call-done = f32[128,128]{1,0:T(8,128)} async-done(((f32[1024,128]{1,0:T(8,128)}), f32[128,128]{1,0:T(8,128)}) %reduce-scatter.30.cloned.1.call-update) | async-done | bytes 65552 | tf_op jit(solution)/shard_map/reduce_scatter | solution.py:460
  1792.2 69.6 %reduce-scatter.36.cloned.1.call-done = f32[384,128]{1,0:T(8,128)} async-done(((f32[384,1024]{1,0:T(8,128)}), f32[384,128]{1,0:T(8,128)}) %reduce-scatter.36.cloned.1.call-update) | async-done | bytes 196624 | tf_op jit(solution)/shard_map/reduce_scatter | solution.py:463
  1861.8 68.3 %reduce-scatter.26.cloned.1.call-done = f32[128,384]{1,0:T(8,128)} async-done(((f32[1024,384]{1,0:T(8,128)}), f32[128,384]{1,0:T(8,128)}) %reduce-scatter.26.cloned.1.call-update) | async-done | bytes 196624 | tf_op jit(solution)/shard_map/reduce_scatter | solution.py:458
  1930.1 68.4 %reduce-scatter.24.cloned.1.call-done = f32[128,384]{1,0:T(8,128)} async-done(((f32[1024,384]{1,0:T(8,128)}), f32[128,384]{1,0:T(8,128)}) %reduce-scatter.24.cloned.1.call-update) | async-done | bytes 196624 | tf_op jit(solution)/shard_map/reduce_scatter | solution.py:457
  (817 shorter events, 447.5 us)
Async XLA Ops:
  8.1 365.2 %all-gather.9.cloned.1.call-start = ((), (), s32[]{:S(2)}) async-start(), calls=%async_computation.15 | async-start | bytes 2621440 | tf_op jit(solution)/shard_map/all_gather | solution.py:264
  53.3 676.7 %copy-start.65 = (f32[1,1024]{1,0:T(1,128)}, f32[1,1024]{1,0:T(1,128)S(1)}, u32[]{:S(2)}) copy-start(f32[1,1024]{1,0:T(1,128)S(1)} %get-tuple-element.1060) | copy-start | bytes 12292
  55.4 175.7 %copy-start.115 = (f32[6]{0:T(128)S(1)}, f32[6]{0:T(128)}, u32[]{:S(2)}) copy-start(f32[6]{0:T(128)} %param.48) | copy-start | bytes 76
  55.4 487.7 %reduce-scatter.16.cloned.1.call-start = ((), (), s32[]{:S(2)}) async-start(), calls=%async_computation.16 | async-start | bytes 2621440 | tf_op jit(solution)/shard_map/reduce_scatter | solution.py:300
  55.8 740.1 %copy-start.105 = (f32[384]{0:T(512)}, f32[384]{0:T(512)S(1)}, u32[]{:S(2)}) copy-start(f32[384]{0:T(512)S(1)} %mul.1168) | copy-start | bytes 4612
  150.4 259.3 %copy-start.61 = (bf16[1024,6]{0,1:T(8,128)(2,1)}, bf16[1024,6]{0,1:T(8,128)(2,1)S(1)}, u32[]{:S(2)}) copy-start(bf16[1024,6]{0,1:T(8,128)(2,1)S(1)} %all_gather.56) | copy-start | bytes 36868
  176.6 201.0 %copy-start.38 = (bf16[1024,64]{0,1:T(8,128)(2,1)}, bf16[1024,64]{0,1:T(8,128)(2,1)S(1)}, u32[]{:S(2)}) copy-start(bf16[1024,64]{0,1:T(8,128)(2,1)S(1)} %all_gather.64) | copy-start | bytes 393220
  202.9 170.4 %copy-start.43 = (bf16[1024,64]{0,1:T(8,128)(2,1)}, bf16[1024,64]{0,1:T(8,128)(2,1)S(1)}, u32[]{:S(2)}) copy-start(bf16[1024,64]{0,1:T(8,128)(2,1)S(1)} %all_gather.63) | copy-start | bytes 393220
  202.9 172.9 %copy-start.108 = (f32[32]{0:T(128)}, f32[32]{0:T(128)S(1)}, u32[]{:S(2)}) copy-start(f32[32]{0:T(128)S(1)} %multiply_power_fusion) | copy-start | bytes 388
  204.2 193.9 %copy-start.77 = (f32[384]{0:T(512)}, f32[384]{0:T(512)S(1)}, u32[]{:S(2)}) copy-start(f32[384]{0:T(512)S(1)} %get-tuple-element.914) | copy-start | bytes 4612
  204.2 193.9 %copy-start.79 = (f32[384]{0:T(512)}, f32[384]{0:T(512)S(1)}, u32[]{:S(2)}) copy-start(f32[384]{0:T(512)S(1)} %get-tuple-element.915) | copy-start | bytes 4612
  204.2 193.9 %copy-start.81 = (f32[384]{0:T(512)}, f32[384]{0:T(512)S(1)}, u32[]{:S(2)}) copy-start(f32[384]{0:T(512)S(1)} %get-tuple-element.916) | copy-start | bytes 4612
  204.2 193.9 %copy-start.83 = (f32[384]{0:T(512)}, f32[384]{0:T(512)S(1)}, u32[]{:S(2)}) copy-start(f32[384]{0:T(512)S(1)} %get-tuple-element.917) | copy-start | bytes 4612
  230.6 276.2 %copy-start.28 = (bf16[128,1024]{1,0:T(8,128)(2,1)}, bf16[128,1024]{1,0:T(8,128)(2,1)S(1)}, u32[]{:S(2)}) copy-start(bf16[128,1024]{1,0:T(8,128)(2,1)S(1)} %all_gather.65) | copy-start | bytes 786436
  231.1 162.6 %copy-start.95 = (f32[256]{0:T(256)}, f32[256]{0:T(256)S(1)}, u32[]{:S(2)}) copy-start(f32[256]{0:T(256)S(1)} %get-tuple-element.909) | copy-start | bytes 3076
  231.1 162.6 %copy-start.97 = (f32[256]{0:T(256)}, f32[256]{0:T(256)S(1)}, u32[]{:S(2)}) copy-start(f32[256]{0:T(256)S(1)} %get-tuple-element.910) | copy-start | bytes 3076
  231.1 162.6 %copy-start.99 = (f32[256]{0:T(256)}, f32[256]{0:T(256)S(1)}, u32[]{:S(2)}) copy-start(f32[256]{0:T(256)S(1)} %get-tuple-element.911) | copy-start | bytes 3076
  231.1 162.6 %copy-start.101 = (f32[256]{0:T(256)}, f32[256]{0:T(256)S(1)}, u32[]{:S(2)}) copy-start(f32[256]{0:T(256)S(1)} %get-tuple-element.912) | copy-start | bytes 3076
  515.4 39.7 %all-gather.15.cloned.1.call-start = ((), (), s32[]{:S(2)}) async-start(), calls=%async_computation.19 | async-start | bytes 1179648 | tf_op jit(solution)/shard_map/all_gather | solution.py:251
  517.1 61.3 %all-gather.11.cloned.1.call-start = ((), (), s32[]{:S(2)}) async-start(), calls=%async_computation.17 | async-start | bytes 2621440 | tf_op jit(solution)/shard_map/all_gather | solution.py:311
  544.4 185.7 %copy-start.75 = (f32[256]{0:T(256)}, f32[256]{0:T(256)S(1)}, u32[]{:S(2)}) copy-start(f32[256]{0:T(256)S(1)} %fusion.311) | copy-start | bytes 3076
  546.4 74.8 %all-gather.13.cloned.1.call-start = ((), (), s32[]{:S(2)}) async-start(), calls=%async_computation.18 | async-start | bytes 1179648 | tf_op jit(solution)/shard_map/all_gather | solution.py:250
  548.1 113.7 %all-gather.17.cloned.1.call-start = ((), (), s32[]{:S(2)}) async-start(), calls=%async_computation.20 | async-start | bytes 1179648 | tf_op jit(solution)/shard_map/all_gather | solution.py:252
  549.8 135.8 %all-gather.19.cloned.1.call-start = ((), (), s32[]{:S(2)}) async-start(), calls=%async_computation.22 | async-start | bytes 2621440 | tf_op jit(solution)/shard_map/all_gather | solution.py:328
  550.6 179.5 %copy-start.89 = (f32[256]{0:T(256)}, f32[256]{0:T(256)S(1)}, u32[]{:S(2)}) copy-start(f32[256]{0:T(256)S(1)} %compare_convert_fusion) | copy-start | bytes 3076
  551.6 176.4 %reduce-scatter.20.cloned.1.call-start = ((), (), s32[]{:S(2)}) async-start(), calls=%async_computation.23 | async-start | bytes 2621440 | tf_op jit(solution)/shard_map/reduce_scatter | solution.py:341
  696.6 58.7 %all-gather.21.cloned.1.call-start = ((), (), s32[]{:S(2)}) async-start(), calls=%async_computation.24 | async-start | bytes 2621440 | tf_op jit(solution)/shard_map/all_gather | solution.py:352
  732.5 458.1 %all-reduce.31.cloned.1.call-start = ((), (), s32[]{:S(2)}) async-start(), calls=%async_computation.37 | async-start | bytes 2097152 | tf_op jit(solution)/shard_map/psum | solution.py:431
  1060.6 162.6 %reduce-scatter.22.cloned.1.call-start = ((), (), s32[]{:S(2)}) async-start(), calls=%async_computation.25 | async-start | bytes 2621440 | tf_op jit(solution)/shard_map/reduce_scatter | solution.py:407
  1076.2 192.6 %reduce-scatter.18.cloned.1.call-start = ((), (), s32[]{:S(2)}) async-start(), calls=%async_computation.21 | async-start | bytes 2621440 | tf_op jit(solution)/shard_map/reduce_scatter | solution.py:318
  1080.4 249.2 %reduce-scatter.44.cloned.1.call-start = ((), (), s32[]{:S(2)}) async-start(), calls=%async_computation.36 | async-start | bytes 2359296 | tf_op jit(solution)/shard_map/reduce_scatter | solution.py:467
  1085.1 315.8 %reduce-scatter.40.cloned.1.call-start = ((), (), s32[]{:S(2)}) async-start(), calls=%async_computation.34 | async-start | bytes 2359296 | tf_op jit(solution)/shard_map/reduce_scatter | solution.py:465
  1089.8 382.6 %reduce-scatter.42.cloned.1.call-start = ((), (), s32[]{:S(2)}) async-start(), calls=%async_computation.35 | async-start | bytes 2359296 | tf_op jit(solution)/shard_map/reduce_scatter | solution.py:466
  1094.4 435.3 %reduce-scatter.28.cloned.1.call-start = ((), (), s32[]{:S(2)}) async-start(), calls=%async_computation.28 | async-start | bytes 36864 | tf_op jit(solution)/shard_map/reduce_scatter | solution.py:459
  1095.5 499.5 %reduce-scatter.32.cloned.1.call-start = ((), (), s32[]{:S(2)}) async-start(), calls=%async_computation.30 | async-start | bytes 294912 | tf_op jit(solution)/shard_map/reduce_scatter | solution.py:461
  1096.7 563.6 %reduce-scatter.34.cloned.1.call-start = ((), (), s32[]{:S(2)}) async-start(), calls=%async_computation.31 | async-start | bytes 294912 | tf_op jit(solution)/shard_map/reduce_scatter | solution.py:462
  1099.0 627.6 %reduce-scatter.38.cloned.1.call-start = ((), (), s32[]{:S(2)}) async-start(), calls=%async_computation.33 | async-start | bytes 589824 | tf_op jit(solution)/shard_map/reduce_scatter | solution.py:464
  1101.9 690.3 %reduce-scatter.30.cloned.1.call-start = ((), (), s32[]{:S(2)}) async-start(), calls=%async_computation.29 | async-start | bytes 589824 | tf_op jit(solution)/shard_map/reduce_scatter | solution.py:460
  1103.6 758.2 %reduce-scatter.36.cloned.1.call-start = ((), (), s32[]{:S(2)}) async-start(), calls=%async_computation.32 | async-start | bytes 1769472 | tf_op jit(solution)/shard_map/reduce_scatter | solution.py:463
  1107.7 822.4 %reduce-scatter.26.cloned.1.call-start = ((), (), s32[]{:S(2)}) async-start(), calls=%async_computation.27 | async-start | bytes 1769472 | tf_op jit(solution)/shard_map/reduce_scatter | solution.py:458
  1111.4 887.0 %reduce-scatter.24.cloned.1.call-start = ((), (), s32[]{:S(2)}) async-start(), calls=%async_computation.26 | async-start | bytes 1769472 | tf_op jit(solution)/shard_map/reduce_scatter | solution.py:457
  1113.9 154.9 %copy-start.11 = (bf16[256,1,1024]{2,0,1:T(8,128)(2,1)S(1)}, bf16[256,1,1024]{2,0,1:T(8,128)(2,1)}, u32[]{:S(2)}) copy-start(bf16[256,1,1024]{2,0,1:T(8,128)(2,1)} %reduce-scatter.16.cloned.1.call-done) | copy-start | bytes 1572868
  1113.9 154.9 %copy-start.16 = (bf16[256,1,1024]{2,0,1:T(8,128)(2,1)S(1)}, bf16[256,1,1024]{2,0,1:T(8,128)(2,1)}, u32[]{:S(2)}) copy-start(bf16[256,1,1024]{2,0,1:T(8,128)(2,1)} %param.30) | copy-start | bytes 1572868
  1113.9 154.9 %copy-start.17 = (bf16[256,1,1024]{2,0,1:T(8,128)(2,1)S(1)}, bf16[256,1,1024]{2,0,1:T(8,128)(2,1)}, u32[]{:S(2)}) copy-start(bf16[256,1,1024]{2,0,1:T(8,128)(2,1)} %reduce-scatter.20.cloned.1.call-done) | copy-start | bytes 1572868
  1113.9 154.9 %copy-start.66 = (f32[1,1024]{1,0:T(1,128)S(1)}, f32[1,1024]{1,0:T(1,128)}, u32[]{:S(2)}) copy-start(f32[1,1024]{1,0:T(1,128)} %copy-done.65) | copy-start | bytes 12292
  1114.0 154.9 %copy-start.76 = (f32[256]{0:T(256)S(1)}, f32[256]{0:T(256)}, u32[]{:S(2)}) copy-start(f32[256]{0:T(256)} %copy-done.75) | copy-start | bytes 3076
  1114.0 154.9 %copy-start.90 = (f32[256]{0:T(256)S(1)}, f32[256]{0:T(256)}, u32[]{:S(2)}) copy-start(f32[256]{0:T(256)} %copy-done.89) | copy-start | bytes 3076
  1114.0 154.9 %copy-start.104 = (f32[256]{0:T(256)S(1)}, f32[256]{0:T(256)}, u32[]{:S(2)}) copy-start(f32[256]{0:T(256)} %copy-done.103) | copy-start | bytes 3076
  (124 other events, 2332.1 us)
Sparse Core Ops, SparseCore 0:
  55.5 18.6 all-gather.8
  515.5 27.4 reduce-scatter.15
  696.7 31.1 reduce-scatter.19
  732.7 22.5 all-gather.20
Sparse Core Ops, SparseCore 1:
  518.6 36.5 all-gather.14
  557.2 21.1 all-gather.10
  580.9 40.2 all-gather.12
  623.8 38.0 all-gather.16
  664.0 21.5 all-gather.18
  1060.7 129.9 all-reduce.30
  1193.0 30.1 reduce-scatter.21
  1225.6 31.2 reduce-scatter.17
  1260.8 68.8 reduce-scatter.43
  1333.8 67.0 reduce-scatter.39
  1404.9 67.4 reduce-scatter.41
  1476.1 53.5 reduce-scatter.27
  1533.4 61.4 reduce-scatter.31
  1598.9 61.5 reduce-scatter.33
  1664.3 62.2 reduce-scatter.37
  1730.5 61.6 reduce-scatter.29
  1796.2 65.5 reduce-scatter.35
  1865.8 64.2 reduce-scatter.25
  1933.9 64.4 reduce-scatter.23
where the time goes:
time: 2020 us; the launch traced here: 2010 us
  waiting for transfers between devices  1040 us (51%)
  blocking collectives  398 us (20%)
  local copies, waits for them, and re-layouts  222 us (11%)
  matrix products  189 us (9%)
  other arithmetic  138 us (7%)
    dynamic_update_slice x24, local copies, waits for them, and re-layouts, state_scan(): final, outs = lax.scan(stepper, start, pieces)  82.4 us
    psum x1, waiting for transfers between devices, body(): lax.psum((state_w_grad, conv_shared_grad, gain_grads, widen(conv_taps_gra...  75.7 us
    reduce_scatter x1, waiting for transfers between devices, body(): lax.psum_scatter(up_w_grad, 'dp', scatter_dimension=0, tiled=True)  71.5 us
    reduce_scatter x1, waiting for transfers between devices, body(): lax.psum_scatter(gate_w_grad, 'dp', scatter_dimension=0, tiled=True)  71.2 us
    reduce_scatter x1, waiting for transfers between devices, body(): lax.psum_scatter(mix_out_grad, 'dp', scatter_dimension=1, tiled=True)  69.6 us
    reduce_scatter x1, waiting for transfers between devices, body(): lax.psum_scatter(input_w_grad, 'dp', scatter_dimension=0, tiled=True)  68.4 us
    reduce_scatter x1, waiting for transfers between devices, body(): lax.psum_scatter(gating_w_grad, 'dp', scatter_dimension=0, tiled=True)  68.3 us
    reduce_scatter x1, waiting for transfers between devices, body(): lax.psum_scatter(att_out_grad, 'dp', scatter_dimension=1, tiled=True)  66.2 us
  transfers between devices with their start and end apart: 23, of which 21 were waited for; matrix products, arithmetic and copies ran while one was open for 4% of the time, Pallas kernels for 0%

commit v1 on v0

v1 whole, which is shorter than its diff:
```python
import jax
import jax.numpy as jnp
from jax import lax
from jax.sharding import PartitionSpec as P

HD = 64
ATT_BLOCK = 512
SPAN = 256
epsilon = 1e-05
rotary_base = 100000000000.0
HIGHEST = lax.Precision.HIGHEST
bf16 = jnp.bfloat16
f32 = jnp.float32


def flip(value, axis, mask):
    size = lax.axis_size(axis)
    return lax.ppermute(value, axis, [(i, i ^ mask) for i in range(size)])


def bits_of(size):
    bits = size.bit_length() - 1
    assert size == 1 << bits
    return bits


def relative_order(size):
    order = [0]
    for bit in reversed(range(bits_of(size))):
        order = order + [k | (1 << bit) for k in order]
    return order


def gather_pieces(own, axis):
    size = lax.axis_size(axis)
    if size > 8:
        held = own
        for bit in reversed(range(bits_of(size))):
            held = jnp.concatenate([held, flip(held, axis, 1 << bit)], axis=0)
        return held
    held = [own]
    for bit in reversed(range(bits_of(size))):
        held = held + [flip(piece, axis, 1 << bit) for piece in held]
    return jnp.concatenate(held, axis=0)


def scatter_sum(whole, axis):
    size = lax.axis_size(axis)
    rows = whole.shape[0] // size
    if size > 8:
        held = whole
        for bit in range(bits_of(size)):
            half = held.shape[0] // 2
            held = held[:half] + flip(held[half:].astype(bf16), axis, 1 << bit).astype(f32)
        return held
    order = relative_order(size)
    held = {k: whole[p * rows : (p + 1) * rows] for p, k in enumerate(order)}
    for bit in range(bits_of(size)):
        mask = 1 << bit
        got = {k ^ mask: flip(v.astype(bf16), axis, mask) for k, v in held.items() if k & mask}
        held = {k: v + got[k].astype(f32) for k, v in held.items() if not k & mask}
    return held[0]


def blocks_by_xor(value, member, size, axis):
    width = value.shape[axis] // size
    return jnp.concatenate(
        [
            lax.dynamic_slice_in_dim(value, (member ^ k) * width, width, axis)
            for k in relative_order(size)
        ],
        axis=axis,
    )


def blocks_back(value, member, size, axis):
    width = value.shape[axis] // size
    where = [0] * size
    for p, k in enumerate(relative_order(size)):
        where[k] = p
    table = jnp.array(where, jnp.int32)
    return jnp.concatenate(
        [
            lax.dynamic_slice_in_dim(value, table[member ^ j] * width, width, axis)
            for j in range(size)
        ],
        axis=axis,
    )


def pick(bit, one, zero):
    return jnp.where(bit == 1, one, zero)


def gather_y(own, y):
    other = flip(own, "tensor", 2)
    return jnp.stack([pick(y, other, own), pick(y, own, other)])


def gather_core(pair, core):
    other = flip(pair, "tensor", 1)
    full = jnp.stack([pick(core, other, pair), pick(core, pair, other)], axis=1)
    return full.reshape((4 * full.shape[2],) + full.shape[3:])


def reduce_core(part, core):
    rows = part.shape[0] // 4
    cut = part.reshape((2, 2, rows) + part.shape[1:])
    sent = pick(core, cut[:, 0], cut[:, 1])
    kept = pick(core, cut[:, 1], cut[:, 0])
    return (kept.astype(f32) + flip(sent, "tensor", 1).astype(f32)).astype(bf16)


def reduce_y_both(pair):
    return pair.astype(f32) + flip(pair, "tensor", 2).astype(f32)


def reduce_y_own(pair, y):
    sent = pick(y, pair[0], pair[1])
    kept = pick(y, pair[1], pair[0])
    return kept.astype(f32) + flip(sent, "tensor", 2).astype(f32)


def rotary_tables(length, size):
    frequency = rotary_base ** (-2.0 * jnp.arange(size // 2, dtype=jnp.float32) / size)
    angles = jnp.arange(length, dtype=jnp.float32)[:, None] * frequency[None, :]
    return (jnp.cos(angles), jnp.sin(angles))


def rotate_pairs(values, cosine, sine):
    half = values.shape[-1] // 2
    first = values[..., :half]
    second = values[..., half:]
    return jnp.concatenate(
        [first * cosine - second * sine, second * cosine + first * sine], axis=-1
    )


def causal_conv(values, taps):
    width = taps.shape[0] - 1
    length = values.shape[0]
    padded = jnp.pad(values, ((width - 1, 0), (0, 0)))
    total = jnp.broadcast_to(taps[width], values.shape)
    for offset in range(width):
        total = total + padded[offset : offset + length] * taps[offset]
    return total


def scan_block(rate, state, block):
    inputs, steps, entry, readout = block
    size = steps.shape[0]
    logs = jnp.cumsum(steps * rate, axis=0)
    order = jnp.arange(size, dtype=jnp.int32)
    causal = (order[:, None] >= order[None, :])[:, :, None]
    spread = jnp.where(causal, logs[:, None, :] - logs[None, :, :], 0.0)
    decay = jnp.where(causal, jnp.exp(spread), 0.0)
    intersection = jnp.dot(readout, entry.T, precision=HIGHEST)
    mixing = decay * intersection[:, :, None] * steps[None, :, :]
    local = jnp.einsum("tsh,shp->thp", mixing, inputs, precision=HIGHEST)
    carried = (
        jnp.einsum("tn,hpn->thp", readout, state, precision=HIGHEST) * jnp.exp(logs)[:, :, None]
    )
    tail = jnp.exp(logs[-1][None, :] - logs) * steps
    fresh = state * jnp.exp(logs[-1])[:, None, None] + jnp.einsum(
        "sh,shp,sn->hpn", tail, inputs, entry, precision=HIGHEST
    )
    return (fresh, local + carried)


def state_scan(inputs, steps, rate, entry, readout):
    length, heads, size = inputs.shape
    blocks = length // SPAN
    pieces = (
        inputs.reshape(blocks, SPAN, heads, size),
        steps.reshape(blocks, SPAN, heads),
        entry.reshape(blocks, SPAN, entry.shape[1]),
        readout.reshape(blocks, SPAN, readout.shape[1]),
    )
    start = jnp.zeros((heads, size, entry.shape[1]), jnp.float32)
    kept_block = jax.checkpoint(scan_block)

    def stepper(state, block):
        return kept_block(rate, state, block)

    final, outs = lax.scan(stepper, start, pieces)
    return outs.reshape(length, heads, size)


def mamba_core(
    ssm_input,
    ssm_gating,
    ssm_states,
    ssm_steps,
    conv_taps,
    conv_shared,
    step_bias,
    decay_log,
    skip_gain,
):
    length = ssm_input.shape[0]
    heads = step_bias.shape[0]
    inputs = jax.nn.silu(causal_conv(ssm_input, conv_taps)).reshape(length, heads, -1)
    shared = jax.nn.silu(causal_conv(ssm_states, conv_shared))
    states = shared.shape[1] // 2
    steps = jax.nn.softplus(ssm_steps + step_bias)
    rate = -jnp.exp(decay_log)
    result = (
        state_scan(inputs, steps, rate, shared[:, :states], shared[:, states:])
        + skip_gain[None, :, None] * inputs
    )
    return result.reshape(length, -1) * jax.nn.silu(ssm_gating)


def swiglu(gate_part, up_part):
    return jax.nn.silu(gate_part) * up_part


def block_scores(block, keys, start, scale):
    length = keys.shape[0]
    scores = jnp.einsum("qcgd,scd->cgqs", block, keys, preferred_element_type=jnp.float32) * scale
    rows = start + jnp.arange(block.shape[0], dtype=jnp.int32)
    allowed = jnp.arange(length, dtype=jnp.int32)[None, :] <= rows[:, None]
    return jnp.where(allowed, scores, -1e30)


def attend_forward(query, keys, values):
    length, heads, size = query.shape
    kv_heads = keys.shape[1]
    groups = heads // kv_heads
    blocks = length // ATT_BLOCK
    scale = size ** (-0.5)
    grouped = query.reshape(blocks, ATT_BLOCK, kv_heads, groups, size)
    starts = jnp.arange(blocks, dtype=jnp.int32) * ATT_BLOCK

    def one_block(item):
        block, start = item
        scores = block_scores(block, keys, start, scale)
        top = jnp.max(scores, axis=-1, keepdims=True)
        expo = jnp.exp(scores - top)
        total = jnp.sum(expo, axis=-1, keepdims=True)
        chance = (expo / total).astype(jnp.bfloat16)
        result = jnp.einsum("cgqs,scd->qcgd", chance, values, preferred_element_type=jnp.float32)
        return (result, (top + jnp.log(total))[..., 0])

    outs, logsum = lax.map(one_block, (grouped, starts))
    return (outs.reshape(length, heads, size), logsum)


def attend_backward(query, keys, values, logsum, grad_out):
    length, heads, size = query.shape
    kv_heads = keys.shape[1]
    groups = heads // kv_heads
    blocks = length // ATT_BLOCK
    scale = size ** (-0.5)
    grouped = query.reshape(blocks, ATT_BLOCK, kv_heads, groups, size)
    grad_grouped = grad_out.reshape(blocks, ATT_BLOCK, kv_heads, groups, size)
    starts = jnp.arange(blocks, dtype=jnp.int32) * ATT_BLOCK

    def one_block(carry, item):
        key_grad, value_grad = carry
        block, start, block_sum, block_grad = item
        scores = block_scores(block, keys, start, scale)
        chance = jnp.exp(scores - block_sum[..., None])
        grad_chance = jnp.einsum(
            "qcgd,scd->cgqs", block_grad, values, preferred_element_type=jnp.float32
        )
        center = jnp.sum(chance * grad_chance, axis=-1, keepdims=True)
        grad_scores = (chance * (grad_chance - center)).astype(jnp.bfloat16)
        query_grad = (
            jnp.einsum("cgqs,scd->qcgd", grad_scores, keys, preferred_element_type=jnp.float32)
            * scale
        )
        key_grad = (
            key_grad
            + jnp.einsum("cgqs,qcgd->scd", grad_scores, block, preferred_element_type=jnp.float32)
            * scale
        )
        value_grad = value_grad + jnp.einsum(
            "cgqs,qcgd->scd",
            chance.astype(jnp.bfloat16),
            block_grad,
            preferred_element_type=jnp.float32,
        )
        return ((key_grad, value_grad), query_grad)

    zeros = jnp.zeros((length, kv_heads, size), jnp.float32)
    (key_grad, value_grad), query_grad = lax.scan(
        one_block, (zeros, zeros), (grouped, starts, logsum, grad_grouped)
    )
    return (query_grad.reshape(length, heads, size), key_grad, value_grad)


def mm(a, b):
    return jnp.dot(a, b, preferred_element_type=f32)


def mm_t(a, b):
    return lax.dot_general(a, b, (((1,), (1,)), ((), ())), preferred_element_type=f32)


def t_mm(a, b):
    return lax.dot_general(a, b, (((0,), (0,)), ((), ())), preferred_element_type=f32)


def body(
    layer_in,
    out_grad,
    lengths,
    mamba_x,
    mamba_z,
    mamba_step,
    query_proj,
    key_proj,
    value_proj,
    mamba_out,
    attend_out,
    mlp_gate,
    mlp_up,
    mlp_down,
    state_proj,
    conv_state,
    norm_gains,
    conv_mamba,
    step_bias,
    decay_log,
    skip_gain,
):
    ranks = lax.axis_size("tensor")
    assert ranks == 4 and layer_in.shape[1] == 1
    rank = lax.axis_index("tensor")
    y, core = rank // 2, rank % 2
    peers = lax.axis_size("dp")
    me = lax.axis_index("dp")
    rows, _, width = layer_in.shape
    length = rows * ranks
    chans = mamba_x.shape[1]
    heads = step_bias.shape[0]
    q_cols, k_cols = query_proj.shape[1], key_proj.shape[1]
    ff = mlp_gate.shape[1]
    d_rows = width // peers
    n2 = state_proj.shape[1]

    own_in = blocks_by_xor(layer_in[:, 0], me, peers, 1)
    own_go = blocks_by_xor(out_grad[:, 0], me, peers, 1)
    in_pair = gather_y(own_in, y)
    in_full = gather_core(in_pair, core)

    taps_own = conv_state.shape[1]
    gains_own = norm_gains.shape[1]
    small = jnp.concatenate([conv_state.reshape(-1), norm_gains.reshape(-1)])
    fill = -small.shape[0] % 128
    small = jnp.pad(small, (0, fill)).reshape(1, -1)
    small = gather_core(gather_y(small, y), core)
    small = gather_pieces(small[None], "dp")
    cut = conv_state.size
    taps_pieces = small[:, :, :cut].reshape(peers, ranks, conv_state.shape[0], taps_own)
    taps_rel = jnp.transpose(taps_pieces, (2, 0, 1, 3)).reshape(conv_state.shape[0], -1)
    conv_shared = blocks_back(taps_rel, me, peers, 1)
    gain_pair = jnp.transpose(
        small[:, :, cut : cut + norm_gains.size].reshape(peers, ranks, 2, gains_own), (2, 0, 1, 3)
    ).reshape(2, width)

    step_pad = -heads % 128
    pack_a = jnp.concatenate(
        [mamba_x.astype(bf16), jnp.pad(mamba_step.astype(bf16), ((0, 0), (0, step_pad)))], axis=1
    )
    w_a = gather_pieces(pack_a, "dp")
    state_own = gather_core(gather_y(state_proj.astype(bf16), y), core)
    w_bc = gather_pieces(state_own, "dp")
    pack_b = jnp.concatenate(
        [item.astype(bf16) for item in (mamba_z, query_proj, key_proj, value_proj)], axis=1
    )
    w_b = gather_pieces(pack_b, "dp")
    pack_o = jnp.concatenate([mamba_out.T.astype(bf16), attend_out.T.astype(bf16)], axis=1)
    w_o = gather_pieces(pack_o, "dp")
    pack_m = jnp.concatenate(
        [mlp_gate.astype(bf16), mlp_up.astype(bf16), mlp_down.T.astype(bf16)], axis=1
    )
    w_m = gather_pieces(pack_m, "dp")

    limit = lengths[0]
    go_pair = gather_y(own_go, y)
    go_full = gather_core(go_pair, core)
    all_valid = jnp.arange(length, dtype=jnp.int32) < limit
    block_valid = all_valid.reshape(2, 2, rows)
    pair_valid = pick(core, block_valid[:, 1], block_valid[:, 0])
    gf = jnp.where(all_valid[:, None], go_full, 0).astype(bf16)

    def norm_parts(values):
        rho = lax.rsqrt(jnp.mean(values * values, axis=-1, keepdims=True) + epsilon)
        return rho

    x_full = in_full.astype(f32)
    rho_one = norm_parts(x_full)
    a1 = (x_full * rho_one * gain_pair[0]).astype(bf16)

    w_x, w_dt = w_a[:, :chans], w_a[:, chans : chans + heads]
    w_z = w_b[:, :chans]
    w_qkv = w_b[:, chans:]
    proj_qkv = mm(a1, w_qkv)
    core_args = (
        mm(a1, w_x),
        mm(a1, w_z),
        mm(a1, w_bc),
        mm(a1, w_dt),
        conv_mamba,
        conv_shared,
        step_bias,
        decay_log,
        skip_gain,
    )
    ssm_out, core_back = jax.vjp(mamba_core, *core_args)
    om = ssm_out.astype(bf16)
    cosine, sine = rotary_tables(length, HD)

    def turn(pre, sign):
        shaped = pre.reshape(length, pre.shape[1] // HD, HD)
        return rotate_pairs(shaped, cosine[:, None, :], sign * sine[:, None, :])

    query = turn(proj_qkv[:, :q_cols], 1.0).astype(bf16)
    keys = turn(proj_qkv[:, q_cols : q_cols + k_cols], 1.0).astype(bf16)
    values = proj_qkv[:, q_cols + k_cols :].reshape(length, -1, HD).astype(bf16)
    att_out, logsum = attend_forward(query, keys, values)
    oa = att_out.reshape(length, -1).astype(bf16)
    mixed_in = jnp.concatenate([om, oa], axis=1)
    m_pair = reduce_y_both(reduce_core(mm_t(mixed_in, w_o).astype(bf16), core))
    r1 = in_pair.astype(f32) + m_pair
    rho_two = norm_parts(r1)
    a2_pair = (r1 * rho_two * gain_pair[1]).astype(bf16)
    a2 = gather_core(a2_pair, core)
    w_gu, w_dn = w_m[:, : 2 * ff], w_m[:, 2 * ff :]
    gate_up = mm(a2, w_gu)
    gate, up = gate_up[:, :ff], gate_up[:, ff:]
    hidden_full, glu_back = jax.vjp(swiglu, gate, up)
    hid = hidden_full.astype(bf16)
    ffn = reduce_y_own(reduce_core(mm_t(hid, w_dn).astype(bf16), core), y)
    r1_own = pick(y, r1[1], r1[0])
    own_valid = pick(y, pair_valid[1], pair_valid[0])
    layer_out = jnp.where(own_valid[:, None], r1_own + ffn, 0.0).astype(bf16)
    layer_out = blocks_back(layer_out, me, peers, 1)[:, None]

    g_hid = mm(gf, w_dn)
    gate_grad, up_grad = glu_back(g_hid)
    g_gu = jnp.concatenate([gate_grad.astype(bf16), up_grad.astype(bf16)], axis=1)
    g_a2_pair = reduce_y_both(reduce_core(mm_t(g_gu, w_gu).astype(bf16), core))
    n_two = r1 * rho_two
    e_two = g_a2_pair * gain_pair[1]
    gf_pair = jnp.where(pair_valid[:, :, None], go_pair.astype(f32), 0.0)
    g_r1 = gf_pair + rho_two * (e_two - n_two * jnp.mean(e_two * n_two, axis=-1, keepdims=True))
    gain_two_pair = jnp.sum(g_a2_pair * n_two, axis=1)
    gain_two_grad = pick(y, gain_two_pair[1], gain_two_pair[0])
    g_m = gather_core(g_r1.astype(bf16), core)
    g_mix = mm(g_m, w_o)
    g_ym = g_mix[:, :chans]
    g_oa = g_mix[:, chans:].astype(bf16)

    mlp_w_grad = jnp.concatenate([t_mm(a2, g_gu), t_mm(gf, hid)], axis=1)
    mlp_sum = scatter_sum(mlp_w_grad, "dp")
    out_sum = scatter_sum(t_mm(g_m, mixed_in), "dp")

    query_grad, keys_grad, values_grad = attend_backward(
        query, keys, values, logsum, g_oa.reshape(length, -1, HD)
    )
    g_qkv = jnp.concatenate(
        [
            turn(query_grad.reshape(length, -1), -1.0).reshape(length, -1),
            turn(keys_grad.reshape(length, -1), -1.0).reshape(length, -1),
            values_grad.reshape(length, -1),
        ],
        axis=1,
    ).astype(bf16)
    (
        g_px,
        g_pz,
        g_pbc,
        g_pdt,
        conv_taps_grad,
        conv_shared_grad,
        bias_grad,
        decay_grad,
        skip_grad,
    ) = core_back(g_ym)
    g_b = jnp.concatenate([g_pz.astype(bf16), g_qkv], axis=1)
    g_a = jnp.concatenate(
        [g_px.astype(bf16), jnp.pad(g_pdt.astype(bf16), ((0, 0), (0, step_pad)))], axis=1
    )
    g_bc = g_pbc.astype(bf16)
    b_sum = scatter_sum(t_mm(a1, g_b), "dp")
    a_sum = scatter_sum(t_mm(a1, g_a), "dp")
    state_part = t_mm(a1, g_bc).astype(bf16).reshape(peers, 4, gains_own, n2)
    state_part = jnp.swapaxes(state_part, 0, 1).reshape(4 * peers * gains_own, n2)
    state_part = reduce_y_own(reduce_core(state_part, core), y)
    state_proj_grad = scatter_sum(state_part, "dp")

    g_a1_part = mm_t(g_b, w_b) + mm_t(g_a, w_a) + mm_t(g_bc, w_bc)
    gain_one_grad = jnp.sum(g_a1_part * (x_full * rho_one), axis=0)
    g_a1 = reduce_y_own(reduce_core(g_a1_part.astype(bf16), core), y)
    x_own = own_in.astype(f32)
    rho_own = norm_parts(x_own)
    n_one = x_own * rho_own
    e_one = g_a1 * gain_pair[0]
    g_r1_own = pick(y, g_r1[1], g_r1[0])
    in_grad = g_r1_own + rho_own * (e_one - n_one * jnp.mean(e_one * n_one, axis=-1, keepdims=True))
    in_grad = blocks_back(in_grad.astype(bf16), me, peers, 1)[:, None]

    gain_grads = blocks_back(jnp.stack([gain_one_grad, gain_two_grad]), me, peers, 1)
    both = jnp.concatenate([conv_shared_grad.reshape(-1), gain_grads.reshape(-1)])
    both_rows = -(-both.shape[0] // 128)
    both = jnp.pad(both, (0, both_rows * 128 - both.shape[0]))
    only = jnp.concatenate([conv_taps_grad.reshape(-1), bias_grad, decay_grad, skip_grad])
    only_count = only.shape[0]
    only = jnp.pad(only, (0, -only_count % 128))
    packed = jnp.concatenate([both, only]).reshape(-1, 128)
    for bit in range(bits_of(peers)):
        packed = packed + flip(packed, "dp", 1 << bit)
    both = packed[:both_rows]
    for mask in (1, 2):
        both = both + flip(both, "tensor", mask)
    both = both.reshape(-1)
    only = packed[both_rows:].reshape(-1)
    conv_state_sum = both[: conv_shared.size].reshape(conv_shared.shape)
    gain_sum = both[conv_shared.size : conv_shared.size + 2 * width].reshape(2, width)
    member = me * ranks + rank
    conv_state_grad = lax.dynamic_slice_in_dim(conv_state_sum, member * taps_own, taps_own, 1)
    norm_gains_grad = lax.dynamic_slice_in_dim(gain_sum, member * gains_own, gains_own, 1)
    cut = conv_taps_grad.size
    conv_mamba_grad = only[:cut].reshape(conv_taps_grad.shape)
    step_bias_grad = only[cut : cut + heads]
    decay_log_grad = only[cut + heads : cut + 2 * heads]
    skip_gain_grad = only[cut + 2 * heads : cut + 3 * heads]

    return (
        layer_out,
        in_grad,
        a_sum[:, :chans],
        b_sum[:, :chans],
        a_sum[:, chans : chans + heads],
        b_sum[:, chans : chans + q_cols],
        b_sum[:, chans + q_cols : chans + q_cols + k_cols],
        b_sum[:, chans + q_cols + k_cols :],
        out_sum[:, :chans].T,
        out_sum[:, chans:].T,
        mlp_sum[:, :ff],
        mlp_sum[:, ff : 2 * ff],
        mlp_sum[:, 2 * ff :].T,
        state_proj_grad,
        conv_state_grad,
        norm_gains_grad,
        conv_mamba_grad,
        step_bias_grad,
        decay_log_grad,
        skip_gain_grad,
    )


def solution(mesh):
    in_specs = (
        P("tensor", "dp", None),
        P("tensor", "dp", None),
        P("dp"),
        P("dp", "tensor"),
        P("dp", "tensor"),
        P("dp", "tensor"),
        P("dp", "tensor"),
        P("dp", "tensor"),
        P("dp", "tensor"),
        P("tensor", "dp"),
        P("tensor", "dp"),
        P("dp", "tensor"),
        P("dp", "tensor"),
        P("tensor", "dp"),
        P(("dp", "tensor"), None),
        P(None, ("dp", "tensor")),
        P(None, ("dp", "tensor")),
        P(None, "tensor"),
        P("tensor"),
        P("tensor"),
        P("tensor"),
    )
    out_specs = (
        P("tensor", "dp", None),
        P("tensor", "dp", None),
        P("dp", "tensor"),
        P("dp", "tensor"),
        P("dp", "tensor"),
        P("dp", "tensor"),
        P("dp", "tensor"),
        P("dp", "tensor"),
        P("tensor", "dp"),
        P("tensor", "dp"),
        P("dp", "tensor"),
        P("dp", "tensor"),
        P("tensor", "dp"),
        P(("dp", "tensor"), None),
        P(None, ("dp", "tensor")),
        P(None, ("dp", "tensor")),
        P(None, "tensor"),
        P("tensor"),
        P("tensor"),
        P("tensor"),
    )
    return jax.shard_map(body, mesh=mesh, in_specs=in_specs, out_specs=out_specs, check_vma=False)
```

time: 2020 us -> 823 us (0.41)
  waiting for transfers between devices: 1040 us -> 190 us
  blocking collectives: 398 us -> 0 us
  starting transfers between devices: 1.35 us -> 83.3 us
  matrix products: 189 us -> 138 us
  other arithmetic: 138 us -> 163 us
    reduce_scatter x15 -> x0, waiting for transfers between devices: 815 us -> none  [the longest x1 71.5 us: body(): lax.psum_scatter(up_w_grad, 'dp', scatter_dimension=0, tiled=True)]
    all_gather x11 -> x0, blocking collectives: 357 us -> none  [the longest x1 43.6 us: body(): lax.all_gather(norm_gains, ('dp', 'tensor'), axis=1, tiled=True)]
    ppermute x0 -> x102, waiting for transfers between devices: none -> 190 us  [flip(): return lax.ppermute(value, axis, [(i, i ^ mask) for i in range(size)])]
    all_gather x7 -> x0, waiting for transfers between devices: 147 us -> none  [the longest x1 38.4 us: body(): lax.all_gather(mlp_gate.astype(low_type), 'dp', axis=0, tiled=True)]
    ppermute x0 -> x102, starting transfers between devices: none -> 83.3 us  [flip(): return lax.ppermute(value, axis, [(i, i ^ mask) for i in range(size)])]
    psum x1 -> x0, waiting for transfers between devices: 75.7 us -> none  [body(): lax.psum((state_w_grad, conv_shared_grad, gain_grads, widen(conv_taps_gra...]
    dot_general x36 -> x20, matrix products: 103 us -> 45.5 us  [the longest x8 16.1 us: mm(): return jnp.dot(a, b, preferred_element_type=f32)]
    psum x1 -> x0, blocking collectives: 40.4 us -> none  [body(): lax.psum((state_w_grad, conv_shared_grad, gain_grads, widen(conv_taps_gra...]
  transfers between devices with their start and end apart: 23 -> 102, of which waited for: 21 -> 51; matrix products, arithmetic and copies ran while one was open for 4% -> 27% of each run, Pallas kernels for 0% -> 0%
where the time goes in v1:
time: 823 us; the launch traced here: 808 us
  local copies, waits for them, and re-layouts  218 us (26%)
  waiting for transfers between devices  190 us (23%)
  other arithmetic  163 us (20%)
  matrix products  138 us (17%)
  starting transfers between devices  83.3 us (10%)
  between operations  14.1 us (2%)
    ppermute x102, waiting for transfers between devices, flip(): return lax.ppermute(value, axis, [(i, i ^ mask) for i in range(size)])  190 us
    ppermute x102, starting transfers between devices, flip(): return lax.ppermute(value, axis, [(i, i ^ mask) for i in range(size)])  83.3 us
    dynamic_update_slice x16, local copies, waits for them, and re-layouts, state_scan(): final, outs = lax.scan(stepper, start, pieces)  79.3 us
    another operation x48, other arithmetic  58.7 us
    unnamed x312, local copies, waits for them, and re-layouts  47.1 us
    dot_general x12, matrix products, scan_block(): local = jnp.einsum('tsh,shp->thp', mixing, inputs, precision=HIGHEST)  29.9 us
  transfers between devices with their start and end apart: 102, of which 51 were waited for; matrix products, arithmetic and copies ran while one was open for 27% of the time, Pallas kernels for 0%

profile of v1, /device:TPU:0, one launch (start us, length us, event | category | flops | bytes accessed | tf_op | source)
XLA Modules:
  0.0 808.5 jit_solution(14231846920671330692)
XLA Ops:
  43.2 4.1 collective-permute-done.4
  72.3 6.2 collective-permute-done.20
  78.7 4.1 collective-permute-done.21
  92.1 6.2 collective-permute-done.27
  100.6 3.6 collective-permute-done.22
  106.3 3.4 collective-permute-done.24
  111.0 3.9 collective-permute-done.26
  130.2 3.9 collective-permute-done.15
  136.5 3.7 collective-permute-done.29
  142.3 4.8 collective-permute-done.31
  171.2 15.6 %while.70 = (s32[]{:T(128)}, bf16[2,512,1,2,64]{1,4,3,2,0:T(8,128)(2,1)}, f32[2,1,2,512]{3,2,1,0:T(2,128)S(1)}, s32[2]{0:T(128)S(1)}, bf16[2,512,1,2,64]{1,4,3,2...) while((s32[]{:T(128)}, ...), condition=%wide.region_8.9_spmd, body=%wide.region_5.8_spmd.sunk | while | flops 281542144 | bytes 17469616 | solution.py:245
  201.4 69.7 %while.73 = (s32[]{:T(128)}, f32[6,64,128]{2,1,0:T(8,128)S(1)}, f32[4,256,6,64]{1,0,3,2:T(4,128)}, f32[4,6,64,128]{3,2,1,0:T(8,128)}, f32[4,256,6]{1,2,0:T(8,128...) while((s32[]{:T(128)}, f32[6,64,128]{2,1,0:T(8,128)S(1)}, ...), condition=%wide.region_4.5_spmd.clone.clone, body=%wide.region_1.4_spmd.clone.clone.sunk | while | flops 707351040 | bytes 5773156 | solution.py:185
  209.2 9.5 %dynamic_update_slice.95 = f32[4,256,6,64]{1,0,3,2:T(4,128)} dynamic-update-slice(f32[4,256,6,64]{1,0,3,2:T(4,128)} %get-tuple-element.1726, f32[1,256,6,64]{1,0,3,2:T(1,128)S(1)} %copy.722, s32[]{:T(128)S(6)} %copy.787, s32[]{:T(128)} %constant.267.clone.1..sunk.2, s32[]{:T(128)} %constant.267.clone.1..sunk.2, s32[]{:T(128)} %constant.267.clone.1..sunk.2) | dynamic-update-slice | bytes 786436 | tf_op jit(solution)/shard_map/jvp()/while/body/jit(dynamic_update_index_in_dim)/dynamic_update_slice | solution.py:185
  226.6 9.5 %dynamic_update_slice.95 = f32[4,256,6,64]{1,0,3,2:T(4,128)} dynamic-update-slice(f32[4,256,6,64]{1,0,3,2:T(4,128)} %get-tuple-element.1726, f32[1,256,6,64]{1,0,3,2:T(1,128)S(1)} %copy.722, s32[]{:T(128)S(6)} %copy.787, s32[]{:T(128)} %constant.267.clone.1..sunk.2, s32[]{:T(128)} %constant.267.clone.1..sunk.2, s32[]{:T(128)} %constant.267.clone.1..sunk.2) | dynamic-update-slice | bytes 786436 | tf_op jit(solution)/shard_map/jvp()/while/body/jit(dynamic_update_index_in_dim)/dynamic_update_slice | solution.py:185
  243.9 9.5 %dynamic_update_slice.95 = f32[4,256,6,64]{1,0,3,2:T(4,128)} dynamic-update-slice(f32[4,256,6,64]{1,0,3,2:T(4,128)} %get-tuple-element.1726, f32[1,256,6,64]{1,0,3,2:T(1,128)S(1)} %copy.722, s32[]{:T(128)S(6)} %copy.787, s32[]{:T(128)} %constant.267.clone.1..sunk.2, s32[]{:T(128)} %constant.267.clone.1..sunk.2, s32[]{:T(128)} %constant.267.clone.1..sunk.2) | dynamic-update-slice | bytes 786436 | tf_op jit(solution)/shard_map/jvp()/while/body/jit(dynamic_update_index_in_dim)/dynamic_update_slice | solution.py:185
  261.2 9.5 %dynamic_update_slice.95 = f32[4,256,6,64]{1,0,3,2:T(4,128)} dynamic-update-slice(f32[4,256,6,64]{1,0,3,2:T(4,128)} %get-tuple-element.1726, f32[1,256,6,64]{1,0,3,2:T(1,128)S(1)} %copy.722, s32[]{:T(128)S(6)} %copy.787, s32[]{:T(128)} %constant.267.clone.1..sunk.2, s32[]{:T(128)} %constant.267.clone.1..sunk.2, s32[]{:T(128)} %constant.267.clone.1..sunk.2) | dynamic-update-slice | bytes 786436 | tf_op jit(solution)/shard_map/jvp()/while/body/jit(dynamic_update_index_in_dim)/dynamic_update_slice | solution.py:185
  278.2 5.2 multiply_convert_fusion.4
  304.0 5.2 collective-permute-done.46
  312.6 13.8 %collective-permute-done.42 = bf16[2,256,1024]{2,1,0:T(8,128)(2,1)S(1)} collective-permute-done((bf16[2,256,1024]{2,1,0:T(8,128)(2,1)S(1)}, bf16[2,256,1024]{2,1,0:T(8,128)(2,1)S(1)}, u32[]{:S(2)}, u32[]{:S(2)}) %collective-permute-start.42) | collective-permute-done | bytes 1048608 | tf_op jit(solution)/shard_map/ppermute | solution.py:18
  344.5 7.4 collective-permute-done.85
  355.0 5.3 collective-permute-done.84
  361.3 7.4 collective-permute-done.82
  376.7 9.6 %collective-permute-done.83 = bf16[128,1536]{0,1:T(8,128)(2,1)S(1)} collective-permute-done((bf16[128,1536]{0,1:T(8,128)(2,1)S(1)}, bf16[128,1536]{0,1:T(8,128)(2,1)S(1)}, u32[]{:S(2)}, u32[]{:S(2)}) %collective-permute-start.83) | collective-permute-done | bytes 393248 | tf_op jit(solution)/shard_map/ppermute | solution.py:18
  392.9 14.7 %collective-permute-done.56 = bf16[2,256,1024]{2,1,0:T(8,128)(2,1)} collective-permute-done((bf16[2,256,1024]{2,1,0:T(8,128)(2,1)}, bf16[2,256,1024]{2,1,0:T(8,128)(2,1)}, u32[]{:S(2)}, u32[]{:S(2)}) %collective-permute-start.56) | collective-permute-done | bytes 1048608 | tf_op jit(solution)/shard_map/ppermute | solution.py:18
  409.8 3.5 fusion.298
  428.1 38.2 %while.71 = (s32[]{:T(128)}, f32[1024,1,64]{0,2,1:T(8,128)}, f32[1024,1,64]{0,2,1:T(8,128)}, f32[2,512,1,2,64]{1,0,4,3,2:T(2,128)}, bf16[2,512,1,2,64]{1,4,3,2,0...) while((s32[]{:T(128)}, f32[1024,1,64]{0,2,1:T(8,128)}, ...), condition=%wide.region_14.15_spmd.clone, body=%wide.region_12.14_spmd.clone.sunk | while | flops 687734272 | bytes 36864172 | solution.py:287
  441.4 5.8 dynamic_update_slice.89
  460.6 5.8 dynamic_update_slice.89
  474.3 5.7 fusion.254
  480.0 3.5 fusion.310
  491.7 175.3 %while.72 = (s32[]{:T(128)}, f32[6]{0:T(128)}, f32[6,64,128]{2,1,0:T(8,128)}, f32[4,256,6,64]{1,0,3,2:T(4,128)}, f32[4,256,6]{1,2,0:T(8,128)}, /*index=5*/f32[4,...) while((s32[]{:T(128)}, f32[6]{0:T(128)}, ...), condition=%wide.region_28.29_spmd.clone, body=%wide.region_15.28_spmd.clone.sunk | while | flops 1670427136 | bytes 15336636 | solution.py:185
  503.5 4.0 fusion.451
  513.9 7.6 reduce-window.74
  525.5 9.5 %dynamic_update_slice.93 = f32[4,256,6,64]{1,0,3,2:T(4,128)} dynamic-update-slice(f32[4,256,6,64]{1,0,3,2:T(4,128)} %get-tuple-element.1807, f32[1,256,6,64]{1,0,3,2:T(1,128)S(1)} %copy.717, s32[]{:T(128)S(6)} %sub.437, s32[]{:T(128)} %constant.267.clone.1..sunk.1, s32[]{:T(128)} %constant.267.clone.1..sunk.1, s32[]{:T(128)} %constant.267.clone.1..sunk.1) | dynamic-update-slice | bytes 786436 | tf_op jit(solution)/shard_map/transpose(jvp())/while/body/jit(dynamic_update_index_in_dim)/dynamic_update_slice | solution.py:185
  547.6 4.0 fusion.451
  557.9 7.6 reduce-window.74
  569.5 9.5 %dynamic_update_slice.93 = f32[4,256,6,64]{1,0,3,2:T(4,128)} dynamic-update-slice(f32[4,256,6,64]{1,0,3,2:T(4,128)} %get-tuple-element.1807, f32[1,256,6,64]{1,0,3,2:T(1,128)S(1)} %copy.717, s32[]{:T(128)S(6)} %sub.437, s32[]{:T(128)} %constant.267.clone.1..sunk.1, s32[]{:T(128)} %constant.267.clone.1..sunk.1, s32[]{:T(128)} %constant.267.clone.1..sunk.1) | dynamic-update-slice | bytes 786436 | tf_op jit(solution)/shard_map/transpose(jvp())/while/body/jit(dynamic_update_index_in_dim)/dynamic_update_slice | solution.py:185
  591.6 4.0 fusion.451
  601.9 7.6 reduce-window.74
  613.5 9.5 %dynamic_update_slice.93 = f32[4,256,6,64]{1,0,3,2:T(4,128)} dynamic-update-slice(f32[4,256,6,64]{1,0,3,2:T(4,128)} %get-tuple-element.1807, f32[1,256,6,64]{1,0,3,2:T(1,128)S(1)} %copy.717, s32[]{:T(128)S(6)} %sub.437, s32[]{:T(128)} %constant.267.clone.1..sunk.1, s32[]{:T(128)} %constant.267.clone.1..sunk.1, s32[]{:T(128)} %constant.267.clone.1..sunk.1) | dynamic-update-slice | bytes 786436 | tf_op jit(solution)/shard_map/transpose(jvp())/while/body/jit(dynamic_update_index_in_dim)/dynamic_update_slice | solution.py:185
  635.6 4.0 fusion.451
  645.9 7.6 reduce-window.74
  657.5 9.5 %dynamic_update_slice.93 = f32[4,256,6,64]{1,0,3,2:T(4,128)} dynamic-update-slice(f32[4,256,6,64]{1,0,3,2:T(4,128)} %get-tuple-element.1807, f32[1,256,6,64]{1,0,3,2:T(1,128)S(1)} %copy.717, s32[]{:T(128)S(6)} %sub.437, s32[]{:T(128)} %constant.267.clone.1..sunk.1, s32[]{:T(128)} %constant.267.clone.1..sunk.1, s32[]{:T(128)} %constant.267.clone.1..sunk.1) | dynamic-update-slice | bytes 786436 | tf_op jit(solution)/shard_map/transpose(jvp())/while/body/jit(dynamic_update_index_in_dim)/dynamic_update_slice | solution.py:185
  675.4 5.8 multiply_reduce_fusion.12
  714.3 4.2 collective-permute-done.99
  728.4 5.2 collective-permute-done.64
  765.7 5.2 collective-permute-done.80
  797.5 4.6 collective-permute-done.73
  (1139 shorter events, 508.3 us)
Async XLA Ops:
  3.4 81.7 %collective-permute-start.35 = (bf16[128,512]{0,1:T(8,128)(2,1)}, bf16[128,512]{0,1:T(8,128)(2,1)S(1)}, u32[]{:S(2)}, u32[]{:S(2)}) collective-permute-start(bf16[128,512]{0,1:T(8,128)(2,1)} %get-tuple-element.1324), channel_id=1, source_target_pairs={{0,8},{4,12},{8,0},{12,4},{16,24},{20,28},{24,16},{28,20},{1,9},{5... | collective-permute-start | bytes 393224 | tf_op jit(solution)/shard_map/ppermute | solution.py:18
  6.4 76.4 %collective-permute-start.34 = (bf16[128,512]{0,1:T(8,128)(2,1)}, bf16[128,512]{0,1:T(8,128)(2,1)}, u32[]{:S(2)}, u32[]{:S(2)}) collective-permute-start(bf16[128,512]{0,1:T(8,128)(2,1)} %get-tuple-element.1324), channel_id=1, source_target_pairs={{0,16},{4,20},{8,24},{12,28},{16,0},{20,4},{24,8},{28,12},{1,17},{... | collective-permute-start | bytes 393224 | tf_op jit(solution)/shard_map/ppermute | solution.py:18
  9.0 109.3 %collective-permute-start.37 = (bf16[128,512]{0,1:T(8,128)(2,1)}, bf16[128,512]{0,1:T(8,128)(2,1)}, u32[]{:S(2)}, u32[]{:S(2)}) collective-permute-start(bf16[128,512]{0,1:T(8,128)(2,1)} %get-tuple-element.1324), channel_id=1, source_target_pairs={{0,4},{4,0},{8,12},{12,8},{16,20},{20,16},{24,28},{28,24},{1,5},{5... | collective-permute-start | bytes 393224 | tf_op jit(solution)/shard_map/ppermute | solution.py:18
  12.1 29.4 %collective-permute-start.2 = (f32[1,128]{1,0:T(1,128)S(1)}, f32[1,128]{1,0:T(1,128)S(1)}, u32[]{:S(2)}, u32[]{:S(2)}) collective-permute-start(f32[1,128]{1,0:T(1,128)S(1)} %fusion.279), channel_id=1, source_target_pairs={{0,2},{1,3},{2,0},{3,1},{4,6},{5,7},{6,4},{7,5},{8,10},{9,11},{10,... | collective-permute-start | bytes 1544 | tf_op jit(solution)/shard_map/ppermute | solution.py:18
  14.4 56.2 %collective-permute-start.18 = (bf16[32,256]{1,0:T(8,128)(2,1)S(1)}, bf16[32,256]{1,0:T(8,128)(2,1)S(1)}, u32[]{:S(2)}, u32[]{:S(2)}) collective-permute-start(bf16[32,256]{1,0:T(8,128)(2,1)S(1)} %convert_element_type.441), channel_id=1, source_target_pairs={{0,2},{1,3},{2,0},{3,1},{4,6},{5,7},{6,4},{7,5},{8,10},{9,11},{10,... | collective-permute-start | bytes 49160 | tf_op jit(solution)/shard_map/ppermute | solution.py:18
  68.9 22.5 %collective-permute-start.12 = (bf16[128,512]{1,0:T(8,128)(2,1)S(1)}, bf16[128,512]{1,0:T(8,128)(2,1)S(1)}, u32[]{:S(2)}, u32[]{:S(2)}) collective-permute-start(bf16[128,512]{1,0:T(8,128)(2,1)S(1)} %get-tuple-element.1322), channel_id=1, source_target_pairs={{0,8},{4,12},{8,0},{12,4},{16,24},{20,28},{24,16},{28,20},{1,9},{5... | collective-permute-start | bytes 393224 | tf_op jit(solution)/shard_map/ppermute | solution.py:18
  82.9 47.2 %collective-permute-start.14 = (bf16[128,512]{1,0:T(8,128)(2,1)S(1)}, bf16[128,512]{1,0:T(8,128)(2,1)S(1)}, u32[]{:S(2)}, u32[]{:S(2)}) collective-permute-start(bf16[128,512]{1,0:T(8,128)(2,1)S(1)} %get-tuple-element.1322), channel_id=1, source_target_pairs={{0,4},{4,0},{8,12},{12,8},{16,20},{20,16},{24,28},{28,24},{1,5},{5... | collective-permute-start | bytes 393224 | tf_op jit(solution)/shard_map/ppermute | solution.py:18
  85.0 14.9 %collective-permute-start.28 = (bf16[128,640]{1,0:T(8,128)(2,1)S(1)}, bf16[128,640]{1,0:T(8,128)(2,1)S(1)}, u32[]{:S(2)}, u32[]{:S(2)}) collective-permute-start(bf16[128,640]{1,0:T(8,128)(2,1)S(1)} %get-tuple-element.1231), channel_id=1, source_target_pairs={{0,8},{4,12},{8,0},{12,4},{16,24},{20,28},{24,16},{28,20},{1,9},{5... | collective-permute-start | bytes 491528 | tf_op jit(solution)/shard_map/ppermute | solution.py:18
  91.4 49.8 %collective-permute-start.30 = (bf16[128,640]{1,0:T(8,128)(2,1)S(1)}, bf16[128,640]{1,0:T(8,128)(2,1)S(1)}, u32[]{:S(2)}, u32[]{:S(2)}) collective-permute-start(bf16[128,640]{1,0:T(8,128)(2,1)S(1)} %get-tuple-element.1231), channel_id=1, source_target_pairs={{0,4},{4,0},{8,12},{12,8},{16,20},{20,16},{24,28},{28,24},{1,5},{5... | collective-permute-start | bytes 491528 | tf_op jit(solution)/shard_map/ppermute | solution.py:18
  114.9 13.8 %collective-permute-start = (bf16[256,1024]{1,0:T(8,128)(2,1)S(1)}, bf16[256,1024]{1,0:T(8,128)(2,1)S(1)}, u32[]{:S(2)}, u32[]{:S(2)}) collective-permute-start(bf16[256,1024]{1,0:T(8,128)(2,1)S(1)} %constant_dynamic-update-slice_fusion), channel_id=1, source_target_pairs={{0,2},{1,3},{2,0},{3,1},{4,6},{5,7},{6,4},{7,5},{8,10},{9,11},{10,... | collective-permute-start | bytes 1572872 | tf_op jit(solution)/shard_map/ppermute | solution.py:18
  124.9 167.3 %collective-permute-start.45 = (bf16[128,1536]{0,1:T(8,128)(2,1)}, bf16[128,1536]{0,1:T(8,128)(2,1)}, u32[]{:S(2)}, u32[]{:S(2)}) collective-permute-start(bf16[128,1536]{0,1:T(8,128)(2,1)} %get-tuple-element.1308), channel_id=1, source_target_pairs={{0,8},{4,12},{8,0},{12,4},{16,24},{20,28},{24,16},{28,20},{1,9},{5... | collective-permute-start | bytes 1179656 | tf_op jit(solution)/shard_map/ppermute | solution.py:18
  130.1 30.2 %collective-permute-start.1 = (bf16[2,256,1024]{2,1,0:T(8,128)(2,1)S(1)}, bf16[2,256,1024]{2,1,0:T(8,128)(2,1)S(1)}, u32[]{:S(2)}, u32[]{:S(2)}) collective-permute-start(bf16[2,256,1024]{2,1,0:T(8,128)(2,1)S(1)} %pad_maximum_fusion.8), channel_id=1, source_target_pairs={{0,1},{1,0},{2,3},{3,2},{4,5},{5,4},{6,7},{7,6},{8,9},{9,8},{10,11... | collective-permute-start | bytes 3145736 | tf_op jit(solution)/shard_map/ppermute | solution.py:18
  135.6 157.6 %collective-permute-start.44 = (bf16[128,1536]{0,1:T(8,128)(2,1)}, bf16[128,1536]{0,1:T(8,128)(2,1)}, u32[]{:S(2)}, u32[]{:S(2)}) collective-permute-start(bf16[128,1536]{0,1:T(8,128)(2,1)} %get-tuple-element.1308), channel_id=1, source_target_pairs={{0,16},{4,20},{8,24},{12,28},{16,0},{20,4},{24,8},{28,12},{1,17},{... | collective-permute-start | bytes 1179656 | tf_op jit(solution)/shard_map/ppermute | solution.py:18
  141.2 9.5 %collective-permute-start.32 = (bf16[128,640]{1,0:T(8,128)(2,1)S(1)}, bf16[128,640]{1,0:T(8,128)(2,1)S(1)}, u32[]{:S(2)}, u32[]{:S(2)}) collective-permute-start(bf16[128,640]{1,0:T(8,128)(2,1)S(1)} %collective-permute-done.28), channel_id=1, source_target_pairs={{0,4},{4,0},{8,12},{12,8},{16,20},{20,16},{24,28},{28,24},{1,5},{5... | collective-permute-start | bytes 491528 | tf_op jit(solution)/shard_map/ppermute | solution.py:18
  157.0 152.3 %collective-permute-start.47 = (bf16[128,1536]{0,1:T(8,128)(2,1)}, bf16[128,1536]{0,1:T(8,128)(2,1)}, u32[]{:S(2)}, u32[]{:S(2)}) collective-permute-start(bf16[128,1536]{0,1:T(8,128)(2,1)} %get-tuple-element.1308), channel_id=1, source_target_pairs={{0,4},{4,0},{8,12},{12,8},{16,20},{20,16},{24,28},{28,24},{1,5},{5... | collective-permute-start | bytes 1179656 | tf_op jit(solution)/shard_map/ppermute | solution.py:18
  159.2 142.4 %collective-permute-start.53 = (bf16[256,1024]{1,0:T(8,128)(2,1)}, bf16[256,1024]{1,0:T(8,128)(2,1)}, u32[]{:S(2)}, u32[]{:S(2)}) collective-permute-start(bf16[256,1024]{1,0:T(8,128)(2,1)} %constant_dynamic-update-slice_fusion.64), channel_id=1, source_target_pairs={{0,2},{1,3},{2,0},{3,1},{4,6},{5,7},{6,4},{7,5},{8,10},{9,11},{10,... | collective-permute-start | bytes 1572872 | tf_op jit(solution)/shard_map/ppermute | solution.py:18
  285.8 12.2 %collective-permute-start.41 = (bf16[2,256,1024]{2,1,0:T(8,128)(2,1)}, bf16[2,256,1024]{2,1,0:T(8,128)(2,1)}, u32[]{:S(2)}, u32[]{:S(2)}) collective-permute-start(bf16[2,256,1024]{2,1,0:T(8,128)(2,1)} %select_bitcast_fusion.9), channel_id=1, source_target_pairs={{0,1},{1,0},{2,3},{3,2},{4,5},{5,4},{6,7},{7,6},{8,9},{9,8},{10,11... | collective-permute-start | bytes 3145736 | tf_op jit(solution)/shard_map/ppermute | solution.py:18
  292.3 35.0 %collective-permute-start.49 = (bf16[128,1536]{0,1:T(8,128)(2,1)}, bf16[128,1536]{0,1:T(8,128)(2,1)S(1)}, u32[]{:S(2)}, u32[]{:S(2)}) collective-permute-start(bf16[128,1536]{0,1:T(8,128)(2,1)} %collective-permute-done.45), channel_id=1, source_target_pairs={{0,4},{4,0},{8,12},{12,8},{16,20},{20,16},{24,28},{28,24},{1,5},{5... | collective-permute-start | bytes 1179656 | tf_op jit(solution)/shard_map/ppermute | solution.py:18
  293.2 19.2 %collective-permute-start.48 = (bf16[128,1536]{0,1:T(8,128)(2,1)}, bf16[128,1536]{0,1:T(8,128)(2,1)S(1)}, u32[]{:S(2)}, u32[]{:S(2)}) collective-permute-start(bf16[128,1536]{0,1:T(8,128)(2,1)} %collective-permute-done.44), channel_id=1, source_target_pairs={{0,4},{4,0},{8,12},{12,8},{16,20},{20,16},{24,28},{28,24},{1,5},{5... | collective-permute-start | bytes 1179656 | tf_op jit(solution)/shard_map/ppermute | solution.py:18
  298.0 11.2 %collective-permute-start.46 = (bf16[128,1536]{0,1:T(8,128)(2,1)}, bf16[128,1536]{0,1:T(8,128)(2,1)S(1)}, u32[]{:S(2)}, u32[]{:S(2)}) collective-permute-start(bf16[128,1536]{0,1:T(8,128)(2,1)} %collective-permute-done.44), channel_id=1, source_target_pairs={{0,8},{4,12},{8,0},{12,4},{16,24},{20,28},{24,16},{28,20},{1,9},{5... | collective-permute-start | bytes 1179656 | tf_op jit(solution)/shard_map/ppermute | solution.py:18
  301.6 24.8 %collective-permute-start.42 = (bf16[2,256,1024]{2,1,0:T(8,128)(2,1)S(1)}, bf16[2,256,1024]{2,1,0:T(8,128)(2,1)S(1)}, u32[]{:S(2)}, u32[]{:S(2)}) collective-permute-start(bf16[2,256,1024]{2,1,0:T(8,128)(2,1)S(1)} %fusion.160), channel_id=1, source_target_pairs={{0,2},{1,3},{2,0},{3,1},{4,6},{5,7},{6,4},{7,5},{8,10},{9,11},{10,... | collective-permute-start | bytes 3145736 | tf_op jit(solution)/shard_map/ppermute | solution.py:18
  309.2 18.4 %collective-permute-start.54 = (bf16[2,256,1024]{2,1,0:T(8,128)(2,1)S(1)}, bf16[2,256,1024]{2,1,0:T(8,128)(2,1)S(1)}, u32[]{:S(2)}, u32[]{:S(2)}) collective-permute-start(bf16[2,256,1024]{2,1,0:T(8,128)(2,1)S(1)} %pad_maximum_fusion.10), channel_id=1, source_target_pairs={{0,1},{1,0},{2,3},{3,2},{4,5},{5,4},{6,7},{7,6},{8,9},{9,8},{10,11... | collective-permute-start | bytes 3145736 | tf_op jit(solution)/shard_map/ppermute | solution.py:18
  309.3 18.1 %collective-permute-start.50 = (bf16[128,1536]{0,1:T(8,128)(2,1)S(1)}, bf16[128,1536]{0,1:T(8,128)(2,1)S(1)}, u32[]{:S(2)}, u32[]{:S(2)}) collective-permute-start(bf16[128,1536]{0,1:T(8,128)(2,1)S(1)} %collective-permute-done.46), channel_id=1, source_target_pairs={{0,4},{4,0},{8,12},{12,8},{16,20},{20,16},{24,28},{28,24},{1,5},{5... | collective-permute-start | bytes 1179656 | tf_op jit(solution)/shard_map/ppermute | solution.py:18
  339.8 12.1 %collective-permute-start.85 = (bf16[128,1536]{0,1:T(8,128)(2,1)S(1)}, bf16[128,1536]{0,1:T(8,128)(2,1)S(1)}, u32[]{:S(2)}, u32[]{:S(2)}) collective-permute-start(bf16[128,1536]{0,1:T(8,128)(2,1)S(1)} %get-tuple-element.1258), channel_id=1, source_target_pairs={{0,4},{4,0},{8,12},{12,8},{16,20},{20,16},{24,28},{28,24},{1,5},{5... | collective-permute-start | bytes 1179656 | tf_op jit(solution)/shard_map/ppermute | solution.py:18
  342.3 29.3 %collective-permute-start.51 = (bf16[2,256,1024]{2,1,0:T(8,128)(2,1)S(1)}, bf16[2,256,1024]{2,1,0:T(8,128)(2,1)S(1)}, u32[]{:S(2)}, u32[]{:S(2)}) collective-permute-start(bf16[2,256,1024]{2,1,0:T(8,128)(2,1)S(1)} %select_bitcast_fusion.6), channel_id=1, source_target_pairs={{0,1},{1,0},{2,3},{3,2},{4,5},{5,4},{6,7},{7,6},{8,9},{9,8},{10,11... | collective-permute-start | bytes 3145736 | tf_op jit(solution)/shard_map/ppermute | solution.py:18
  342.4 17.9 %collective-permute-start.84 = (bf16[128,1536]{0,1:T(8,128)(2,1)S(1)}, bf16[128,1536]{0,1:T(8,128)(2,1)S(1)}, u32[]{:S(2)}, u32[]{:S(2)}) collective-permute-start(bf16[128,1536]{0,1:T(8,128)(2,1)S(1)} %get-tuple-element.1259), channel_id=1, source_target_pairs={{0,4},{4,0},{8,12},{12,8},{16,20},{20,16},{24,28},{28,24},{1,5},{5... | collective-permute-start | bytes 1179656 | tf_op jit(solution)/shard_map/ppermute | solution.py:18
  343.5 25.2 %collective-permute-start.82 = (bf16[128,1536]{0,1:T(8,128)(2,1)S(1)}, bf16[128,1536]{0,1:T(8,128)(2,1)S(1)}, u32[]{:S(2)}, u32[]{:S(2)}) collective-permute-start(bf16[128,1536]{0,1:T(8,128)(2,1)S(1)} %get-tuple-element.1260), channel_id=1, source_target_pairs={{0,4},{4,0},{8,12},{12,8},{16,20},{20,16},{24,28},{28,24},{1,5},{5... | collective-permute-start | bytes 1179656 | tf_op jit(solution)/shard_map/ppermute | solution.py:18
  352.0 16.7 %collective-permute-start.86 = (bf16[128,1536]{0,1:T(8,128)(2,1)S(1)}, bf16[128,1536]{0,1:T(8,128)(2,1)S(1)}, u32[]{:S(2)}, u32[]{:S(2)}) collective-permute-start(bf16[128,1536]{0,1:T(8,128)(2,1)S(1)} %fusion.211), channel_id=1, source_target_pairs={{0,8},{4,12},{8,0},{12,4},{16,24},{20,28},{24,16},{28,20},{1,9},{5... | collective-permute-start | bytes 1179656 | tf_op jit(solution)/shard_map/ppermute | solution.py:18
  354.9 18.8 %collective-permute-start.55 = (bf16[2,256,1024]{2,1,0:T(8,128)(2,1)S(1)}, bf16[2,256,1024]{2,1,0:T(8,128)(2,1)S(1)}, u32[]{:S(2)}, u32[]{:S(2)}) collective-permute-start(bf16[2,256,1024]{2,1,0:T(8,128)(2,1)S(1)} %select_bitcast_fusion.3), channel_id=1, source_target_pairs={{0,1},{1,0},{2,3},{3,2},{4,5},{5,4},{6,7},{7,6},{8,9},{9,8},{10,11... | collective-permute-start | bytes 3145736 | tf_op jit(solution)/shard_map/ppermute | solution.py:18
  360.3 16.4 %collective-permute-start.81 = (bf16[128,1536]{0,1:T(8,128)(2,1)S(1)}, bf16[128,1536]{0,1:T(8,128)(2,1)S(1)}, u32[]{:S(2)}, u32[]{:S(2)}) collective-permute-start(bf16[128,1536]{0,1:T(8,128)(2,1)S(1)} %get-tuple-element.1257), channel_id=1, source_target_pairs={{0,4},{4,0},{8,12},{12,8},{16,20},{20,16},{24,28},{28,24},{1,5},{5... | collective-permute-start | bytes 1179656 | tf_op jit(solution)/shard_map/ppermute | solution.py:18
  368.9 17.4 %collective-permute-start.83 = (bf16[128,1536]{0,1:T(8,128)(2,1)S(1)}, bf16[128,1536]{0,1:T(8,128)(2,1)S(1)}, u32[]{:S(2)}, u32[]{:S(2)}) collective-permute-start(bf16[128,1536]{0,1:T(8,128)(2,1)S(1)} %get-tuple-element.1251), channel_id=1, source_target_pairs={{0,8},{4,12},{8,0},{12,4},{16,24},{20,28},{24,16},{28,20},{1,9},{5... | collective-permute-start | bytes 1179656 | tf_op jit(solution)/shard_map/ppermute | solution.py:18
  369.3 18.6 %collective-permute-start.87 = (bf16[128,1536]{0,1:T(8,128)(2,1)S(1)}, bf16[128,1536]{0,1:T(8,128)(2,1)S(1)}, u32[]{:S(2)}, u32[]{:S(2)}) collective-permute-start(bf16[128,1536]{0,1:T(8,128)(2,1)S(1)} %get-tuple-element.1252), channel_id=1, source_target_pairs={{0,16},{4,20},{8,24},{12,28},{16,0},{20,4},{24,8},{28,12},{1,17},{... | collective-permute-start | bytes 1179656 | tf_op jit(solution)/shard_map/ppermute | solution.py:18
  373.0 18.5 %collective-permute-start.52 = (bf16[256,1024]{1,0:T(8,128)(2,1)}, bf16[256,1024]{1,0:T(8,128)(2,1)}, u32[]{:S(2)}, u32[]{:S(2)}) collective-permute-start(bf16[256,1024]{1,0:T(8,128)(2,1)} %select_bitcast_fusion.15), channel_id=1, source_target_pairs={{0,2},{1,3},{2,0},{3,1},{4,6},{5,7},{6,4},{7,5},{8,10},{9,11},{10,... | collective-permute-start | bytes 1572872 | tf_op jit(solution)/shard_map/ppermute | solution.py:18
  375.4 32.2 %collective-permute-start.56 = (bf16[2,256,1024]{2,1,0:T(8,128)(2,1)}, bf16[2,256,1024]{2,1,0:T(8,128)(2,1)}, u32[]{:S(2)}, u32[]{:S(2)}) collective-permute-start(bf16[2,256,1024]{2,1,0:T(8,128)(2,1)} %fusion.158), channel_id=1, source_target_pairs={{0,2},{1,3},{2,0},{3,1},{4,6},{5,7},{6,4},{7,5},{8,10},{9,11},{10,... | collective-permute-start | bytes 3145736 | tf_op jit(solution)/shard_map/ppermute | solution.py:18
  690.5 73.1 %collective-permute-start.74 = (bf16[128,512]{1,0:T(8,128)(2,1)}, bf16[128,512]{1,0:T(8,128)(2,1)}, u32[]{:S(2)}, u32[]{:S(2)}) collective-permute-start(bf16[128,512]{1,0:T(8,128)(2,1)} %get-tuple-element.1283), channel_id=1, source_target_pairs={{0,4},{4,0},{8,12},{12,8},{16,20},{20,16},{24,28},{28,24},{1,5},{5... | collective-permute-start | bytes 393224 | tf_op jit(solution)/shard_map/ppermute | solution.py:18
  691.0 34.1 %collective-permute-start.78 = (bf16[128,512]{1,0:T(8,128)(2,1)}, bf16[128,512]{1,0:T(8,128)(2,1)}, u32[]{:S(2)}, u32[]{:S(2)}) collective-permute-start(bf16[128,512]{1,0:T(8,128)(2,1)} %get-tuple-element.1284), channel_id=1, source_target_pairs={{0,4},{4,0},{8,12},{12,8},{16,20},{20,16},{24,28},{28,24},{1,5},{5... | collective-permute-start | bytes 393224 | tf_op jit(solution)/shard_map/ppermute | solution.py:18
  692.5 49.2 %collective-permute-start.77 = (bf16[128,512]{1,0:T(8,128)(2,1)}, bf16[128,512]{1,0:T(8,128)(2,1)}, u32[]{:S(2)}, u32[]{:S(2)}) collective-permute-start(bf16[128,512]{1,0:T(8,128)(2,1)} %get-tuple-element.1285), channel_id=1, source_target_pairs={{0,4},{4,0},{8,12},{12,8},{16,20},{20,16},{24,28},{28,24},{1,5},{5... | collective-permute-start | bytes 393224 | tf_op jit(solution)/shard_map/ppermute | solution.py:18
  693.0 33.8 %collective-permute-start.75 = (bf16[128,512]{1,0:T(8,128)(2,1)}, bf16[128,512]{1,0:T(8,128)(2,1)}, u32[]{:S(2)}, u32[]{:S(2)}) collective-permute-start(bf16[128,512]{1,0:T(8,128)(2,1)} %get-tuple-element.1286), channel_id=1, source_target_pairs={{0,4},{4,0},{8,12},{12,8},{16,20},{20,16},{24,28},{28,24},{1,5},{5... | collective-permute-start | bytes 393224 | tf_op jit(solution)/shard_map/ppermute | solution.py:18
  723.5 13.8 %collective-permute-start.71 = (bf16[128,640]{0,1:T(8,128)(2,1)}, bf16[128,640]{0,1:T(8,128)(2,1)S(1)}, u32[]{:S(2)}, u32[]{:S(2)}) collective-permute-start(bf16[128,640]{0,1:T(8,128)(2,1)} %get-tuple-element.1280), channel_id=1, source_target_pairs={{0,4},{4,0},{8,12},{12,8},{16,20},{20,16},{24,28},{28,24},{1,5},{5... | collective-permute-start | bytes 491528 | tf_op jit(solution)/shard_map/ppermute | solution.py:18
  726.8 9.3 %collective-permute-start.61 = (bf16[128,512]{0,1:T(8,128)(2,1)}, bf16[128,512]{0,1:T(8,128)(2,1)S(1)}, u32[]{:S(2)}, u32[]{:S(2)}) collective-permute-start(bf16[128,512]{0,1:T(8,128)(2,1)} %get-tuple-element.1290), channel_id=1, source_target_pairs={{0,4},{4,0},{8,12},{12,8},{16,20},{20,16},{24,28},{28,24},{1,5},{5... | collective-permute-start | bytes 393224 | tf_op jit(solution)/shard_map/ppermute | solution.py:18
  737.3 60.2 %collective-permute-start.67 = (bf16[128,640]{0,1:T(8,128)(2,1)}, bf16[128,640]{0,1:T(8,128)(2,1)}, u32[]{:S(2)}, u32[]{:S(2)}) collective-permute-start(bf16[128,640]{0,1:T(8,128)(2,1)} %get-tuple-element.1279), channel_id=1, source_target_pairs={{0,4},{4,0},{8,12},{12,8},{16,20},{20,16},{24,28},{28,24},{1,5},{5... | collective-permute-start | bytes 491528 | tf_op jit(solution)/shard_map/ppermute | solution.py:18
  738.9 14.1 %collective-permute-start.70 = (bf16[128,640]{0,1:T(8,128)(2,1)S(1)}, bf16[128,640]{0,1:T(8,128)(2,1)S(1)}, u32[]{:S(2)}, u32[]{:S(2)}) collective-permute-start(bf16[128,640]{0,1:T(8,128)(2,1)S(1)} %get-tuple-element.1281), channel_id=1, source_target_pairs={{0,4},{4,0},{8,12},{12,8},{16,20},{20,16},{24,28},{28,24},{1,5},{5... | collective-permute-start | bytes 491528 | tf_op jit(solution)/shard_map/ppermute | solution.py:18
  750.5 22.1 %collective-permute-start.60 = (bf16[128,512]{0,1:T(8,128)(2,1)S(1)}, bf16[128,512]{0,1:T(8,128)(2,1)S(1)}, u32[]{:S(2)}, u32[]{:S(2)}) collective-permute-start(bf16[128,512]{0,1:T(8,128)(2,1)S(1)} %copy-done.72), channel_id=1, source_target_pairs={{0,4},{4,0},{8,12},{12,8},{16,20},{20,16},{24,28},{28,24},{1,5},{5... | collective-permute-start | bytes 393224 | tf_op jit(solution)/shard_map/ppermute | solution.py:18
  753.0 10.7 %collective-permute-start.76 = (bf16[128,512]{1,0:T(8,128)(2,1)S(1)}, bf16[128,512]{1,0:T(8,128)(2,1)S(1)}, u32[]{:S(2)}, u32[]{:S(2)}) collective-permute-start(bf16[128,512]{1,0:T(8,128)(2,1)S(1)} %get-tuple-element.1263), channel_id=1, source_target_pairs={{0,8},{4,12},{8,0},{12,4},{16,24},{20,28},{24,16},{28,20},{1,9},{5... | collective-permute-start | bytes 393224 | tf_op jit(solution)/shard_map/ppermute | solution.py:18
  763.7 25.2 %collective-permute-start.58 = (bf16[2,256,1024]{2,1,0:T(8,128)(2,1)}, bf16[2,256,1024]{2,1,0:T(8,128)(2,1)S(1)}, u32[]{:S(2)}, u32[]{:S(2)}) collective-permute-start(bf16[2,256,1024]{2,1,0:T(8,128)(2,1)} %select_bitcast_fusion), channel_id=1, source_target_pairs={{0,1},{1,0},{2,3},{3,2},{4,5},{5,4},{6,7},{7,6},{8,9},{9,8},{10,11... | collective-permute-start | bytes 3145736 | tf_op jit(solution)/shard_map/ppermute | solution.py:18
  763.7 9.8 %collective-permute-start.62 = (bf16[128,512]{0,1:T(8,128)(2,1)S(1)}, bf16[128,512]{0,1:T(8,128)(2,1)S(1)}, u32[]{:S(2)}, u32[]{:S(2)}) collective-permute-start(bf16[128,512]{0,1:T(8,128)(2,1)S(1)} %get-tuple-element.1265), channel_id=1, source_target_pairs={{0,8},{4,12},{8,0},{12,4},{16,24},{20,28},{24,16},{28,20},{1,9},{5... | collective-permute-start | bytes 393224 | tf_op jit(solution)/shard_map/ppermute | solution.py:18
  785.0 12.5 %collective-permute-start.69 = (bf16[128,640]{0,1:T(8,128)(2,1)}, bf16[128,640]{0,1:T(8,128)(2,1)S(1)}, u32[]{:S(2)}, u32[]{:S(2)}) collective-permute-start(bf16[128,640]{0,1:T(8,128)(2,1)} %get-tuple-element.1261), channel_id=1, source_target_pairs={{0,8},{4,12},{8,0},{12,4},{16,24},{20,28},{24,16},{28,20},{1,9},{5... | collective-permute-start | bytes 491528 | tf_op jit(solution)/shard_map/ppermute | solution.py:18
  794.8 10.7 %collective-permute-start.59 = (bf16[256,1024]{1,0:T(8,128)(2,1)S(1)}, bf16[256,1024]{1,0:T(8,128)(2,1)S(1)}, u32[]{:S(2)}, u32[]{:S(2)}) collective-permute-start(bf16[256,1024]{1,0:T(8,128)(2,1)S(1)} %select_bitcast_fusion.12), channel_id=1, source_target_pairs={{0,2},{1,3},{2,0},{3,1},{4,6},{5,7},{6,4},{7,5},{8,10},{9,11},{10,... | collective-permute-start | bytes 1572872 | tf_op jit(solution)/shard_map/ppermute | solution.py:18
  (225 other events, 2074.9 us)
